TPU v7x, 128 devices: a whole 4x4x4 slice. The times are simulated.
128 devices in a mesh: section: 16 (over z, x_lo, core), tensor: 8 (over x_hi, y).
Axes of the slice: x: 4 (x_hi: 2, x_lo: 2; x = x_hi * 2 + x_lo), y: 4, z: 4, core: 2. Of those that a mesh axis runs over, the one named last changes fastest.
Arguments:
- fwd_input: float32 [16, 256, 1024], P('section', 'tensor'), may hold values from -6 to 6
- out_grad: float32 [16, 256, 1024], P('section', 'tensor'), may hold values from -6 to 6
- w_inner: float32 [16, 1024, 16384], P('section', None, 'tensor'), may hold values from -0.1875 to 0.1875
- w_outer: float32 [16, 16384, 1024], P('section', 'tensor'), may hold values from -0.046875 to 0.046875
- lent_saved: float32 [16, 256, 16384], P('section', None, 'tensor'), may hold values from -6 to 6
Outputs:
- fwd_output: float32 [16, 256, 1024], P('section', 'tensor')
- in_grad: float32 [16, 256, 1024], P('section', 'tensor')
- lent_new: float32 [16, 256, 16384], P('section', None, 'tensor')
All inputs are finite; a program needn't handle non-finite values.
Results may differ from a plain program's by a relative error of at most 0.00007.
Values sent between devices are 32-bit elements; how exact they have to be, the bound alone decides.
No kernel may reach another device: no remote copies, remote signals or barrier semaphores. Data moves between devices by JAX's collectives and lax.ppermute only.
A program may use at most 128 MiB of HBM per device.

v0:
```python
import jax
import jax.numpy as jnp
from jax import lax
from jax.sharding import PartitionSpec as P


def from_partner(value, axis, distance):
    mask = 2**distance
    pairs = [(source, source ^ mask) for source in range(lax.axis_size(axis))]
    return lax.ppermute(value, axis, pairs)


def from_behind(value, axis, by):
    length = lax.axis_size(axis)
    return lax.ppermute(value, axis, [(i, (i + by) % length) for i in range(length)])


def gelu_exact(value):
    return 0.5 * value * (1.0 + jax.scipy.special.erf(value / jnp.sqrt(2.0).astype(value.dtype)))


def gelu_slope(value):
    cumul = 0.5 * (1.0 + jax.scipy.special.erf(value / jnp.sqrt(2.0).astype(value.dtype)))
    dense = jnp.exp(-0.5 * value * value) / jnp.sqrt(2.0 * jnp.pi).astype(value.dtype)
    return cumul + value * dense


def forward_pass(x_rows, w_first, w_second):
    pre = jnp.dot(
        lax.all_gather(x_rows, "tensor", axis=0, tiled=True),
        w_first,
        precision=lax.Precision.HIGHEST,
        preferred_element_type=jnp.float32,
    )
    active = gelu_exact(pre)
    summed = lax.psum_scatter(
        jnp.dot(
            active, w_second, precision=lax.Precision.HIGHEST, preferred_element_type=jnp.float32
        ),
        "tensor",
        scatter_dimension=0,
        tiled=True,
    )
    return (x_rows + summed, pre)


def backward_pass(g_rows, w_first, w_second, old_pre):
    d_act = lax.dot_general(
        lax.all_gather(g_rows, "tensor", axis=0, tiled=True),
        w_second,
        (((1,), (1,)), ((), ())),
        precision=lax.Precision.HIGHEST,
        preferred_element_type=jnp.float32,
    )
    d_pre = d_act * gelu_slope(old_pre)
    summed = lax.psum_scatter(
        lax.dot_general(
            d_pre,
            w_first,
            (((1,), (1,)), ((), ())),
            precision=lax.Precision.HIGHEST,
            preferred_element_type=jnp.float32,
        ),
        "tensor",
        scatter_dimension=0,
        tiled=True,
    )
    return g_rows + summed


def shards(fwd_input, out_grad, w_inner, w_outer, lent_saved):
    x_rows = fwd_input[0]
    g_rows = out_grad[0]
    w_first = w_inner[0]
    w_second = w_outer[0]
    held = lent_saved[0]
    top_bit = lax.axis_size("section").bit_length() - 2
    out, pre = forward_pass(x_rows, w_first, w_second)
    given, old_pre = from_partner((pre, held), "section", top_bit)
    grad = backward_pass(g_rows, w_first, w_second, old_pre)
    moved_out = from_behind(out, "section", 1)
    moved_grad = from_behind(grad, "section", -1)
    return (moved_out[None], moved_grad[None], given[None])


def solution(mesh):
    return jax.shard_map(
        shards,
        mesh=mesh,
        in_specs=(
            P("section", "tensor", None),
            P("section", "tensor", None),
            P("section", None, "tensor"),
            P("section", "tensor", None),
            P("section", None, "tensor"),
        ),
        out_specs=(
            P("section", "tensor", None),
            P("section", "tensor", None),
            P("section", None, "tensor"),
        ),
        check_vma=False,
    )
```

profile of v0, /device:TPU:1, one launch (start us, length us, event | category | flops | bytes accessed | tf_op | source)
XLA Modules:
  0.0 272.0 jit_solution(2340988541288902736)
XLA Ops:
  7.2 0.0 all-gather.5.cloned.1.call-start
  7.2 0.7 all-gather.5.cloned.1.call-update
  7.9 0.0 all-gather.7.cloned.1.call-start
  7.9 0.7 all-gather.7.cloned.1.call-update
  8.7 0.0 reduce-scatter.3.cloned.1.call-start
  8.7 4.5 %collective-permute-start.1 = (f32[256,2048]{1,0:T(8,128)}, f32[256,2048]{1,0:T(8,128)}, u32[]{:S(2)}, u32[]{:S(2)}) collective-permute-start(f32[256,2048]{1,0:T(8,128)} %bitcast.26), channel_id=1, source_target_pairs={{0,64},{8,72},{16,80},{24,88},{32,96},{40,104},{48,112},{56,120},{... | collective-permute-start | bytes 6291464 | tf_op jit(solution)/shard_map/ppermute | solution.py:10
  13.2 45.3 %all-gather.5.cloned.1.call-done = f32[1,256,1024]{2,1,0:T(8,128)} async-done(((f32[1,32,1024]{2,1,0:T(8,128)}), f32[1,256,1024]{2,1,0:T(8,128)}) %all-gather.5.cloned.1.call-update) | async-done | bytes 1048592 | tf_op jit(solution)/shard_map/all_gather | solution.py:30
  58.5 0.0 copy-start
  58.5 10.0 %fusion.6 = f32[256,2048]{1,0:T(8,128)S(1)} fusion(f32[1,1024,2048]{2,1,0:T(8,128)} %param.7, f32[1,256,1024]{2,1,0:T(8,128)} %all-gather.5.cloned.1.call-done), kind=kOutput, calls=%fused_computation.6 | convolution fusion | flops 6442450944 | bytes 11534336 | tf_op jit(solution)/shard_map/dot_general | solution.py:29
  68.6 0.0 copy-done
  68.6 8.4 %fusion.2 = f32[256,1024]{1,0:T(8,128)} fusion(f32[1,2048,1024]{2,1,0:T(8,128)S(1)} %copy-done, f32[256,2048]{1,0:T(8,128)S(1)} %fusion.6), kind=kOutput, calls=%fused_computation.2 | convolution fusion | flops 6444548096 | bytes 11534336 | tf_op jit(solution)/shard_map/dot_general | solution.py:37
  77.0 0.0 reduce-scatter.3.cloned.1.call-update
  77.0 0.2 reduce-scatter.5.cloned.1.call-start
  77.2 28.6 %all-gather.7.cloned.1.call-done = f32[1,256,1024]{2,1,0:T(8,128)} async-done(((f32[1,32,1024]{2,1,0:T(8,128)}), f32[1,256,1024]{2,1,0:T(8,128)}) %all-gather.7.cloned.1.call-update) | async-done | bytes 1048592 | tf_op jit(solution)/shard_map/all_gather | solution.py:49
  105.8 10.0 %fusion = f32[256,2048]{1,0:T(8,128)S(1)} fusion(f32[1,2048,1024]{2,1,0:T(8,128)} %param.8, f32[1,256,1024]{2,1,0:T(8,128)} %all-gather.7.cloned.1.call-done), kind=kOutput, calls=%fused_computation | convolution fusion | flops 6442450944 | bytes 11534336 | tf_op jit(solution)/shard_map/dot_general | solution.py:48
  115.8 0.0 copy-start.1
  115.8 0.0 copy-start.2
  115.8 0.0 collective-permute-done.1
  115.9 12.7 %fusion.4 = f32[256,1024]{1,0:T(8,128)} fusion(f32[1,1024,2048]{2,1,0:T(8,128)} %param.7, f32[256,2048]{1,0:T(8,128)S(1)} %fusion, f32[256,2048]{1,0:T(8,128)} %collective-permute-done.1), kind=kOutput, calls=%fused_computation.4 | convolution fusion | flops 6447169536 | bytes 13631488 | tf_op jit(solution)/shard_map/dot_general | solution.py:57
  128.6 0.0 reduce-scatter.5.cloned.1.call-update
  128.6 2.9 %collective-permute-start.3 = (f32[256,2048]{1,0:T(8,128)S(1)}, f32[256,2048]{1,0:T(8,128)}, u32[]{:S(2)}, u32[]{:S(2)}) collective-permute-start(f32[256,2048]{1,0:T(8,128)S(1)} %fusion.6), channel_id=1, source_target_pairs={{0,64},{8,72},{16,80},{24,88},{32,96},{40,104},{48,112},{56,120},{... | collective-permute-start | bytes 6291464 | tf_op jit(solution)/shard_map/ppermute | solution.py:10
  131.6 48.9 %reduce-scatter.3.cloned.1.call-done = f32[32,1024]{1,0:T(8,128)} async-done(((f32[256,1024]{1,0:T(8,128)}), f32[32,1024]{1,0:T(8,128)}) %reduce-scatter.3.cloned.1.call-update) | async-done | bytes 131088 | tf_op jit(solution)/shard_map/reduce_scatter | solution.py:36
  180.5 0.0 copy-done.1
  180.5 0.9 bitcast_add_fusion.1
  181.4 2.5 collective-permute-start
  183.9 70.6 %reduce-scatter.5.cloned.1.call-done = f32[32,1024]{1,0:T(8,128)} async-done(((f32[256,1024]{1,0:T(8,128)}), f32[32,1024]{1,0:T(8,128)}) %reduce-scatter.5.cloned.1.call-update) | async-done | bytes 131088 | tf_op jit(solution)/shard_map/reduce_scatter | solution.py:56
  254.5 0.0 copy-done.2
  254.5 0.9 bitcast_add_fusion
  255.4 2.6 collective-permute-start.2
  258.0 0.0 collective-permute-done.3
  258.0 0.0 collective-permute-done
  258.0 3.0 %collective-permute-done.2 = f32[32,1024]{1,0:T(8,128)S(1)} collective-permute-done((f32[32,1024]{1,0:T(8,128)S(1)}, f32[32,1024]{1,0:T(8,128)S(1)}, u32[]{:S(2)}, u32[]{:S(2)}) %collective-permute-start.2) | collective-permute-done | bytes 131104 | tf_op jit(solution)/shard_map/ppermute | solution.py:15
  261.0 0.7 copy.11
  261.7 0.7 copy.12
  262.3 3.1 %copy.13 = f32[1,256,2048]{2,1,0:T(8,128)} copy(f32[1,256,2048]{2,1,0:T(8,128)} %bitcast.9) | data formatting | bytes 4194304
Async XLA Ops:
  7.2 51.4 %all-gather.5.cloned.1.call-start = ((), (), s32[]{:S(2)}) async-start(), calls=%async_computation.4 | async-start | bytes 1179648 | tf_op jit(solution)/shard_map/all_gather | solution.py:30
  7.9 97.9 %all-gather.7.cloned.1.call-start = ((), (), s32[]{:S(2)}) async-start(), calls=%async_computation.5 | async-start | bytes 1179648 | tf_op jit(solution)/shard_map/all_gather | solution.py:49
  8.7 171.9 %reduce-scatter.3.cloned.1.call-start = ((), (), s32[]{:S(2)}) async-start(), calls=%async_computation.2 | async-start | bytes 1179648 | tf_op jit(solution)/shard_map/reduce_scatter | solution.py:36
  8.7 107.2 %collective-permute-start.1 = (f32[256,2048]{1,0:T(8,128)}, f32[256,2048]{1,0:T(8,128)}, u32[]{:S(2)}, u32[]{:S(2)}) collective-permute-start(f32[256,2048]{1,0:T(8,128)} %bitcast.26), channel_id=1, source_target_pairs={{0,64},{8,72},{16,80},{24,88},{32,96},{40,104},{48,112},{56,120},{... | collective-permute-start | bytes 6291464 | tf_op jit(solution)/shard_map/ppermute | solution.py:10
  58.5 10.1 %copy-start = (f32[1,2048,1024]{2,1,0:T(8,128)S(1)}, f32[1,2048,1024]{2,1,0:T(8,128)}, u32[]{:S(2)}) copy-start(f32[1,2048,1024]{2,1,0:T(8,128)} %param.8) | copy-start | bytes 25165828
  77.0 177.5 %reduce-scatter.5.cloned.1.call-start = ((), (), s32[]{:S(2)}) async-start(), calls=%async_computation.3 | async-start | bytes 1179648 | tf_op jit(solution)/shard_map/reduce_scatter | solution.py:56
  115.8 64.7 %copy-start.1 = (f32[1,32,1024]{2,1,0:T(8,128)S(1)}, f32[1,32,1024]{2,1,0:T(8,128)}, u32[]{:S(2)}) copy-start(f32[1,32,1024]{2,1,0:T(8,128)} %param.5) | copy-start | bytes 393220
  115.8 138.7 %copy-start.2 = (f32[1,32,1024]{2,1,0:T(8,128)S(1)}, f32[1,32,1024]{2,1,0:T(8,128)}, u32[]{:S(2)}) copy-start(f32[1,32,1024]{2,1,0:T(8,128)} %param.6) | copy-start | bytes 393220
  128.6 129.4 %collective-permute-start.3 = (f32[256,2048]{1,0:T(8,128)S(1)}, f32[256,2048]{1,0:T(8,128)}, u32[]{:S(2)}, u32[]{:S(2)}) collective-permute-start(f32[256,2048]{1,0:T(8,128)S(1)} %fusion.6), channel_id=1, source_target_pairs={{0,64},{8,72},{16,80},{24,88},{32,96},{40,104},{48,112},{56,120},{... | collective-permute-start | bytes 6291464 | tf_op jit(solution)/shard_map/ppermute | solution.py:10
  181.4 76.6 %collective-permute-start = (f32[32,1024]{1,0:T(8,128)S(1)}, f32[32,1024]{1,0:T(8,128)S(1)}, u32[]{:S(2)}, u32[]{:S(2)}) collective-permute-start(f32[32,1024]{1,0:T(8,128)S(1)} %bitcast_add_fusion.1), channel_id=1, source_target_pairs={{0,8},{8,16},{16,24},{24,32},{32,40},{40,48},{48,56},{56,64},{64,7... | collective-permute-start | bytes 393224 | tf_op jit(solution)/shard_map/ppermute | solution.py:15
  255.4 5.6 %collective-permute-start.2 = (f32[32,1024]{1,0:T(8,128)S(1)}, f32[32,1024]{1,0:T(8,128)S(1)}, u32[]{:S(2)}, u32[]{:S(2)}) collective-permute-start(f32[32,1024]{1,0:T(8,128)S(1)} %bitcast_add_fusion), channel_id=1, source_target_pairs={{0,120},{8,0},{16,8},{24,16},{32,24},{40,32},{48,40},{56,48},{64,5... | collective-permute-start | bytes 393224 | tf_op jit(solution)/shard_map/ppermute | solution.py:15
Sparse Core Ops, SparseCore 0:
  10.4 48.1 all-gather.4
  60.9 44.9 all-gather.6
  110.0 70.4 reduce-scatter.2
  184.4 70.0 reduce-scatter.4
where the time goes:
time: 272 us
  waiting for transfers between devices  198 us (73%)
  matrix products  41.1 us (15%)
  between operations  13.8 us (5%)
  starting transfers between devices  12.8 us (5%)
  local copies, waits for them, and re-layouts  4.46 us (2%)
    reduce_scatter x1, waiting for transfers between devices, backward_pass(): lax.psum_scatter(lax.dot_general(d_pre, w_first, (((1,), (1,)), ((), ()))...  70.6 us
    reduce_scatter x1, waiting for transfers between devices, forward_pass(): lax.psum_scatter(jnp.dot(active, w_second, precision=lax.Precision.HIGHES...  48.9 us
    all_gather x1, waiting for transfers between devices, forward_pass(): lax.all_gather(x_rows, 'tensor', axis=0, tiled=True)  45.3 us
    all_gather x1, waiting for transfers between devices, backward_pass(): lax.all_gather(g_rows, 'tensor', axis=0, tiled=True)  28.6 us
    dot_general x1, matrix products, backward_pass(): lax.dot_general(d_pre, w_first, (((1,), (1,)), ((), ())), precision=lax.P...  12.7 us
    dot_general x1, matrix products, forward_pass(): jnp.dot(lax.all_gather(x_rows, 'tensor', axis=0, tiled=True), w_first, pr...  10 us
    dot_general x1, matrix products, backward_pass(): lax.dot_general(lax.all_gather(g_rows, 'tensor', axis=0, tiled=True), w_s...  9.97 us
    dot_general x1, matrix products, forward_pass(): jnp.dot(active, w_second, precision=lax.Precision.HIGHEST, preferred_elem...  8.38 us
  transfers between devices with their start and end apart: 8, of which 5 were waited for; matrix products, arithmetic and copies ran while one was open for 16% of the time, Pallas kernels for 0%

commit v1 on v0

v1 whole, which is shorter than its diff:
```python
import functools
import math

import jax
import jax.numpy as jnp
from jax import lax
from jax.experimental import pallas as pl
from jax.experimental.pallas import tpu as pltpu
from jax.sharding import PartitionSpec as P

F32 = jnp.float32
BF16 = jnp.bfloat16
ROOT_HALF = math.sqrt(0.5)
DENSITY = 1.0 / math.sqrt(2.0 * math.pi)
VMEM_LIMIT = 48 * 1024 * 1024


def shifted(value, by):
    length = lax.axis_size("section")
    return lax.ppermute(value, "section", [(i, (i + by) % length) for i in range(length)])


def across(value, mask):
    length = lax.axis_size("tensor")
    return lax.ppermute(value, "tensor", [(i, i ^ mask) for i in range(length)])


def halves(value):
    high = value.astype(BF16)
    return high, (value - high.astype(F32)).astype(BF16)


def product(left, right, contract):
    dims = (contract, ((), ()))
    (lh, ll), (rh, rl) = left, right
    dot = functools.partial(lax.dot_general, dimension_numbers=dims, preferred_element_type=F32)
    return dot(lh, rh) + (dot(lh, rl) + dot(ll, rh))


PLAIN = ((1,), (0,))
TURNED = ((1,), (1,))


def gelu(value):
    return 0.5 * value * (1.0 + lax.erf(value * ROOT_HALF))


def gelu_slope(value):
    return 0.5 * (1.0 + lax.erf(value * ROOT_HALF)) + value * (jnp.exp(-0.5 * value * value) * DENSITY)


def forward_kernel(parts, rows, *refs):
    place_ref, refs = refs[0], refs[1:]
    got, refs = refs[:parts], refs[parts:]
    first_ref, second_ref, pre_ref, dact_ref, sum_ref, xh, xl, gh, gl = refs

    @pl.when(pl.program_id(0) == 0)
    def _():
        place = place_ref[0]
        for mask in range(parts):
            at = pl.ds(pl.multiple_of((place ^ mask) * rows, rows), rows)
            high, low = halves(got[mask][:rows])
            xh[at, :] = high
            xl[at, :] = low
            high, low = halves(got[mask][rows:])
            gh[at, :] = high
            gl[at, :] = low
        sum_ref[...] = jnp.zeros_like(sum_ref)

    pre = product((xh[...], xl[...]), halves(first_ref[...]), PLAIN)
    pre_ref[...] = pre
    second = halves(second_ref[...])
    dact_ref[...] = product((gh[...], gl[...]), second, TURNED)
    sum_ref[...] += product(halves(gelu(pre)), second, PLAIN)


def forward(place, got, w_first, w_second, tile):
    parts, rows, depth = len(got), got[0].shape[0] // 2, got[0].shape[1]
    hidden = w_first.shape[1]
    total = parts * rows
    whole = pl.BlockSpec((2 * rows, depth), lambda j, s: (0, 0))
    column = pl.BlockSpec((total, tile), lambda j, s: (0, j))
    return pl.pallas_call(
        functools.partial(forward_kernel, parts, rows),
        out_shape=(
            jax.ShapeDtypeStruct((total, hidden), F32),
            jax.ShapeDtypeStruct((total, hidden), F32),
            jax.ShapeDtypeStruct((total, depth), F32),
        ),
        grid_spec=pltpu.PrefetchScalarGridSpec(
            num_scalar_prefetch=1,
            grid=(hidden // tile,),
            in_specs=[whole] * parts
            + [
                pl.BlockSpec((depth, tile), lambda j, s: (0, j)),
                pl.BlockSpec((tile, depth), lambda j, s: (j, 0)),
            ],
            out_specs=[column, column, pl.BlockSpec((total, depth), lambda j, s: (0, 0))],
            scratch_shapes=[pltpu.VMEM((total, depth), BF16)] * 4,
        ),
        compiler_params=pltpu.CompilerParams(
            dimension_semantics=("arbitrary",), vmem_limit_bytes=VMEM_LIMIT
        ),
        cost_estimate=pl.CostEstimate(
            flops=18 * total * depth * hidden,
            bytes_accessed=4 * (2 * depth * hidden + 2 * total * hidden + 3 * total * depth),
            transcendentals=total * hidden,
        ),
        name="forward",
    )(place, *got, w_first, w_second)


def backward_kernel(parts, rows, *refs):
    place_ref, dact_ref, old_ref, first_ref, fsum_ref = refs[:5]
    outs, acc = refs[5 : 5 + parts], refs[5 + parts]

    @pl.when(pl.program_id(0) == 0)
    def _():
        acc[...] = jnp.zeros_like(acc)

    hidden_grad = dact_ref[...] * gelu_slope(old_ref[...])
    acc[...] += product(halves(hidden_grad), halves(first_ref[...]), TURNED)

    @pl.when(pl.program_id(0) == pl.num_programs(0) - 1)
    def _():
        place = place_ref[0]
        for mask in range(parts):
            at = pl.ds(pl.multiple_of((place ^ mask) * rows, rows), rows)
            outs[mask][:rows] = fsum_ref[at, :]
            outs[mask][rows:] = acc[at, :]


def backward(place, d_act, old_pre, w_first, fwd_sum, parts, tile):
    total, hidden = d_act.shape
    depth = w_first.shape[0]
    rows = total // parts
    column = pl.BlockSpec((total, tile), lambda j, s: (0, j))
    return pl.pallas_call(
        functools.partial(backward_kernel, parts, rows),
        out_shape=[jax.ShapeDtypeStruct((2 * rows, depth), F32)] * parts,
        grid_spec=pltpu.PrefetchScalarGridSpec(
            num_scalar_prefetch=1,
            grid=(hidden // tile,),
            in_specs=[
                column,
                column,
                pl.BlockSpec((depth, tile), lambda j, s: (0, j)),
                pl.BlockSpec((total, depth), lambda j, s: (0, 0)),
            ],
            out_specs=[pl.BlockSpec((2 * rows, depth), lambda j, s: (0, 0))] * parts,
            scratch_shapes=[pltpu.VMEM((total, depth), F32)],
        ),
        compiler_params=pltpu.CompilerParams(
            dimension_semantics=("arbitrary",), vmem_limit_bytes=VMEM_LIMIT
        ),
        cost_estimate=pl.CostEstimate(
            flops=6 * total * depth * hidden,
            bytes_accessed=4 * (depth * hidden + 2 * total * hidden + 3 * total * depth),
            transcendentals=2 * total * hidden,
        ),
        name="backward",
    )(place, d_act, old_pre, w_first, fwd_sum)


def shards(fwd_input, out_grad, w_inner, w_outer, lent_saved):
    parts = lax.axis_size("tensor")
    half = lax.axis_size("section") // 2
    rows = fwd_input.shape[1]
    place = lax.axis_index("tensor").astype(jnp.int32)[None]

    old_pre = shifted(lent_saved[0], half)
    both = jnp.concatenate([fwd_input[0], out_grad[0]], axis=0)
    got = [both] + [across(both, mask) for mask in range(1, parts)]
    pre, d_act, fwd_sum = forward(place, got, w_inner[0], w_outer[0], 256)
    given = shifted(pre, half)
    sums = backward(place, d_act, old_pre, w_inner[0], fwd_sum, parts, 256)
    total = both + sums[0]
    for mask in range(1, parts):
        total = total + across(sums[mask], mask)
    moved_out = shifted(total[:rows], 1)
    moved_grad = shifted(total[rows:], -1)
    return (moved_out[None], moved_grad[None], given[None])


def solution(mesh):
    return jax.shard_map(
        shards,
        mesh=mesh,
        in_specs=(
            P("section", "tensor", None),
            P("section", "tensor", None),
            P("section", None, "tensor"),
            P("section", "tensor", None),
            P("section", None, "tensor"),
        ),
        out_specs=(
            P("section", "tensor", None),
            P("section", "tensor", None),
            P("section", None, "tensor"),
        ),
        check_vma=False,
    )
```

time: 272 us -> 115 us (0.42)
  waiting for transfers between devices: 198 us -> 34 us
  matrix products: 41.1 us -> 0 us
  starting transfers between devices: 12.8 us -> 48.5 us
  Pallas kernels: 0 us -> 24.5 us
  between operations: 13.8 us -> 0.68 us
    reduce_scatter x2 -> x0, waiting for transfers between devices: 120 us -> none  [the longest x1 70.6 us: backward_pass(): lax.psum_scatter(lax.dot_general(d_pre, w_first, (((1,), (1,)), ((), ()))...]
    all_gather x2 -> x0, waiting for transfers between devices: 73.9 us -> none  [the longest x1 45.3 us: forward_pass(): lax.all_gather(x_rows, 'tensor', axis=0, tiled=True)]
    dot_general x4 -> x0, matrix products: 41.1 us -> none  [the longest x1 12.7 us: backward_pass(): lax.dot_general(d_pre, w_first, (((1,), (1,)), ((), ())), precision=lax.P...]
    ppermute x4 -> x18, starting transfers between devices: 12.5 us -> 48.5 us  [the longest x14 29.9 us: across(): return lax.ppermute(value, 'tensor', [(i, i ^ mask) for i in range(length)])]
    ppermute x4 -> x18, waiting for transfers between devices: 3.02 us -> 34 us  [the longest x14 30.4 us: across(): return lax.ppermute(value, 'tensor', [(i, i ^ mask) for i in range(length)])]
    pallas_call x0 -> x2, Pallas kernels: none -> 24.5 us  [the longest x1 15.2 us: forward(): pl.pallas_call(functools.partial(forward_kernel, parts, rows), out_shape=...]
  transfers between devices with their start and end apart: 8 -> 18, of which waited for: 5 -> 10; matrix products, arithmetic and copies ran while one was open for 16% -> 1% of each run, Pallas kernels for 0% -> 22%
where the time goes in v1:
time: 115 us; the launch traced here: 113 us
  starting transfers between devices  48.5 us (42%)
  waiting for transfers between devices  34 us (30%)
  Pallas kernels  24.5 us (21%)
  local copies, waits for them, and re-layouts  4.25 us (4%)
    ppermute x14, waiting for transfers between devices, across(): return lax.ppermute(value, 'tensor', [(i, i ^ mask) for i in range(length)])  30.4 us
    ppermute x14, starting transfers between devices, across(): return lax.ppermute(value, 'tensor', [(i, i ^ mask) for i in range(length)])  29.9 us
    ppermute x4, starting transfers between devices, shifted(): lax.ppermute(value, 'section', [(i, (i + by) % length) for i in range(len...  18.6 us
    pallas_call x1, Pallas kernels, forward(): pl.pallas_call(functools.partial(forward_kernel, parts, rows), out_shape=...  15.2 us
    pallas_call x1, Pallas kernels, backward(): pl.pallas_call(functools.partial(backward_kernel, parts, rows), out_shape...  9.38 us
    unnamed x9, local copies, waits for them, and re-layouts  4.23 us
    ppermute x4, waiting for transfers between devices, shifted(): lax.ppermute(value, 'section', [(i, (i + by) % length) for i in range(len...  3.56 us
  transfers between devices with their start and end apart: 18, of which 10 were waited for; matrix products, arithmetic and copies ran while one was open for 1% of the time, Pallas kernels for 22%

profile of v1, /device:TPU:1, one launch (start us, length us, event | category | flops | bytes accessed | tf_op | source)
XLA Modules:
  0.0 113.1 jit_solution(16784380130691144388)
XLA Ops:
  0.6 4.5 %collective-permute-start.7 = (f32[256,2048]{1,0:T(8,128)}, f32[256,2048]{1,0:T(8,128)}, u32[]{:S(2)}, u32[]{:S(2)}) collective-permute-start(f32[256,2048]{1,0:T(8,128)} %bitcast.19), channel_id=1, source_target_pairs={{0,64},{8,72},{16,80},{24,88},{32,96},{40,104},{48,112},{56,120},{... | collective-permute-start | bytes 6291464 | tf_op jit(solution)/shard_map/ppermute | solution.py:20
  5.1 1.0 pad_maximum_fusion.refs_1_
  6.1 5.3 %collective-permute-start.6 = (f32[64,1024]{1,0:T(8,128)S(1)}, f32[64,1024]{1,0:T(8,128)S(1)}, u32[]{:S(2)}, u32[]{:S(2)}) collective-permute-start(f32[64,1024]{1,0:T(8,128)S(1)} %pad_maximum_fusion.refs_1_), channel_id=1, source_target_pairs={{0,7},{1,6},{2,5},{3,4},{4,3},{5,2},{6,1},{7,0},{8,15},{9,14},{10,... | collective-permute-start | bytes 786440 | tf_op jit(solution)/shard_map/ppermute | solution.py:25
  11.4 0.3 collective-permute-start.5
  11.7 2.6 %collective-permute-start.4 = (f32[64,1024]{1,0:T(8,128)S(1)}, f32[64,1024]{1,0:T(8,128)S(1)}, u32[]{:S(2)}, u32[]{:S(2)}) collective-permute-start(f32[64,1024]{1,0:T(8,128)S(1)} %pad_maximum_fusion.refs_1_), channel_id=1, source_target_pairs={{0,5},{1,4},{2,7},{3,6},{4,1},{5,0},{6,3},{7,2},{8,13},{9,12},{10,... | collective-permute-start | bytes 786440 | tf_op jit(solution)/shard_map/ppermute | solution.py:25
  14.3 0.4 collective-permute-start.3
  14.8 2.2 %collective-permute-done.6.refs_8_ = f32[64,1024]{1,0:T(8,128)S(1)} collective-permute-done((f32[64,1024]{1,0:T(8,128)S(1)}, f32[64,1024]{1,0:T(8,128)S(1)}, u32[]{:S(2)}, u32[]{:S(2)}) %collective-permute-start.6) | collective-permute-done | bytes 262176 | tf_op jit(solution)/shard_map/ppermute | solution.py:25
  16.9 2.5 %collective-permute-start.2 = (f32[64,1024]{1,0:T(8,128)S(1)}, f32[64,1024]{1,0:T(8,128)S(1)}, u32[]{:S(2)}, u32[]{:S(2)}) collective-permute-start(f32[64,1024]{1,0:T(8,128)S(1)} %pad_maximum_fusion.refs_1_), channel_id=1, source_target_pairs={{0,3},{1,2},{2,1},{3,0},{4,7},{5,6},{6,5},{7,4},{8,11},{9,10},{10,... | collective-permute-start | bytes 786440 | tf_op jit(solution)/shard_map/ppermute | solution.py:25
  19.4 3.5 %collective-permute-done.5.refs_7_ = f32[64,1024]{1,0:T(8,128)S(1)} collective-permute-done((f32[64,1024]{1,0:T(8,128)S(1)}, f32[64,1024]{1,0:T(8,128)S(1)}, u32[]{:S(2)}, u32[]{:S(2)}) %collective-permute-start.5) | collective-permute-done | bytes 262176 | tf_op jit(solution)/shard_map/ppermute | solution.py:25
  22.9 2.4 %collective-permute-start.1 = (f32[64,1024]{1,0:T(8,128)S(1)}, f32[64,1024]{1,0:T(8,128)S(1)}, u32[]{:S(2)}, u32[]{:S(2)}) collective-permute-start(f32[64,1024]{1,0:T(8,128)S(1)} %pad_maximum_fusion.refs_1_), channel_id=1, source_target_pairs={{0,2},{1,3},{2,0},{3,1},{4,6},{5,7},{6,4},{7,5},{8,10},{9,11},{10,... | collective-permute-start | bytes 786440 | tf_op jit(solution)/shard_map/ppermute | solution.py:25
  25.3 2.8 %collective-permute-done.4.refs_6_ = f32[64,1024]{1,0:T(8,128)S(1)} collective-permute-done((f32[64,1024]{1,0:T(8,128)S(1)}, f32[64,1024]{1,0:T(8,128)S(1)}, u32[]{:S(2)}, u32[]{:S(2)}) %collective-permute-start.4) | collective-permute-done | bytes 262176 | tf_op jit(solution)/shard_map/ppermute | solution.py:25
  28.2 1.3 %collective-permute-start = (f32[64,1024]{1,0:T(8,128)S(1)}, f32[64,1024]{1,0:T(8,128)S(1)}, u32[]{:S(2)}, u32[]{:S(2)}) collective-permute-start(f32[64,1024]{1,0:T(8,128)S(1)} %pad_maximum_fusion.refs_1_), channel_id=1, source_target_pairs={{0,1},{1,0},{2,3},{3,2},{4,5},{5,4},{6,7},{7,6},{8,9},{9,8},{10,11... | collective-permute-start | bytes 786440 | tf_op jit(solution)/shard_map/ppermute | solution.py:25
  29.4 4.5 %collective-permute-done.3.refs_5_ = f32[64,1024]{1,0:T(8,128)S(1)} collective-permute-done((f32[64,1024]{1,0:T(8,128)S(1)}, f32[64,1024]{1,0:T(8,128)S(1)}, u32[]{:S(2)}, u32[]{:S(2)}) %collective-permute-start.3) | collective-permute-done | bytes 262176 | tf_op jit(solution)/shard_map/ppermute | solution.py:25
  34.0 0.0 collective-permute-done.2.refs_4_
  34.0 0.7 collective-permute-done.1.refs_3_
  34.6 5.2 %collective-permute-done.refs_2_ = f32[64,1024]{1,0:T(8,128)S(1)} collective-permute-done((f32[64,1024]{1,0:T(8,128)S(1)}, f32[64,1024]{1,0:T(8,128)S(1)}, u32[]{:S(2)}, u32[]{:S(2)}) %collective-permute-start) | collective-permute-done | bytes 262176 | tf_op jit(solution)/shard_map/ppermute | solution.py:25
  39.9 15.2 %forward.1 = (f32[256,2048]{1,0:T(8,128)S(1)}, f32[256,2048]{1,0:T(8,128)}, f32[256,1024]{1,0:T(8,128)S(1)}) custom-call(s32[1]{0:T(128)} %bitcast.2.refs_0_, f32[64,1024]{1,0:T(8,128)S(1)} %pad_maximum_fusion.refs_1_, f32[64,1024]{1,0:T(8,128)S(1)} %collective-permute-done.refs_2_, f32[64,1024]{1,0:T(8,128)S(1)} %collective-permute-done.1.refs_3_, ...), custom_call_target="tpu_custom_call" | custom-call | flops 9663676416 | bytes 24117248 | tf_op jit(solution)/shard_map/forward/pallas_call | solution.py:83
  55.0 0.3 collective-permute-start.17
  55.3 0.0 collective-permute-done.7.refs_2_
  55.4 0.0 copy-start
  55.4 1.6 %copy-done = f32[256,2048]{1,0:T(8,128)S(1)} copy-done((f32[256,2048]{1,0:T(8,128)S(1)}, f32[256,2048]{1,0:T(8,128)}, u32[]{:S(2)}) %copy-start) | copy-done | bytes 2097176
  56.9 0.0 copy-start.1
  56.9 0.0 copy-start.2
  56.9 9.4 %backward.1 = (f32[64,1024]{1,0:T(8,128)S(1)}, f32[64,1024]{1,0:T(8,128)S(1)}, f32[64,1024]{1,0:T(8,128)S(1)}, f32[64,1024]{1,0:T(8,128)S(1)}, f32[64,1024]{1,0:...) custom-call(s32[1]{0:T(128)} %bitcast.2.refs_0_, f32[256,2048]{1,0:T(8,128)S(1)} %copy-done, ...), custom_call_target="tpu_custom_call" | custom-call | flops 3221225472 | bytes 15728640 | tf_op jit(solution)/shard_map/backward/pallas_call | solution.py:138
  66.3 1.3 %collective-permute-start.8 = (f32[64,1024]{1,0:T(8,128)S(1)}, f32[64,1024]{1,0:T(8,128)S(1)}, u32[]{:S(2)}, u32[]{:S(2)}) collective-permute-start(f32[64,1024]{1,0:T(8,128)S(1)} %get-tuple-element.17), channel_id=1, source_target_pairs={{0,1},{1,0},{2,3},{3,2},{4,5},{5,4},{6,7},{7,6},{8,9},{9,8},{10,11... | collective-permute-start | bytes 786440 | tf_op jit(solution)/shard_map/ppermute | solution.py:25
  67.6 0.6 collective-permute-start.9
  68.3 2.0 %collective-permute-start.10 = (f32[64,1024]{1,0:T(8,128)S(1)}, f32[64,1024]{1,0:T(8,128)S(1)}, u32[]{:S(2)}, u32[]{:S(2)}) collective-permute-start(f32[64,1024]{1,0:T(8,128)S(1)} %get-tuple-element.19), channel_id=1, source_target_pairs={{0,3},{1,2},{2,1},{3,0},{4,7},{5,6},{6,5},{7,4},{8,11},{9,10},{10,... | collective-permute-start | bytes 786440 | tf_op jit(solution)/shard_map/ppermute | solution.py:25
  70.3 2.7 %collective-permute-start.11 = (f32[64,1024]{1,0:T(8,128)S(1)}, f32[64,1024]{1,0:T(8,128)S(1)}, u32[]{:S(2)}, u32[]{:S(2)}) collective-permute-start(f32[64,1024]{1,0:T(8,128)S(1)} %get-tuple-element.20), channel_id=1, source_target_pairs={{0,4},{1,5},{2,6},{3,7},{4,0},{5,1},{6,2},{7,3},{8,12},{9,13},{10,... | collective-permute-start | bytes 786440 | tf_op jit(solution)/shard_map/ppermute | solution.py:25
  73.0 0.0 collective-permute-done.8
  73.0 3.3 %collective-permute-start.12 = (f32[64,1024]{1,0:T(8,128)S(1)}, f32[64,1024]{1,0:T(8,128)S(1)}, u32[]{:S(2)}, u32[]{:S(2)}) collective-permute-start(f32[64,1024]{1,0:T(8,128)S(1)} %get-tuple-element.21), channel_id=1, source_target_pairs={{0,5},{1,4},{2,7},{3,6},{4,1},{5,0},{6,3},{7,2},{8,13},{9,12},{10,... | collective-permute-start | bytes 786440 | tf_op jit(solution)/shard_map/ppermute | solution.py:25
  76.3 3.1 %collective-permute-done.9 = f32[64,1024]{1,0:T(8,128)S(1)} collective-permute-done((f32[64,1024]{1,0:T(8,128)S(1)}, f32[64,1024]{1,0:T(8,128)S(1)}, u32[]{:S(2)}, u32[]{:S(2)}) %collective-permute-start.9) | collective-permute-done | bytes 262176 | tf_op jit(solution)/shard_map/ppermute | solution.py:25
  79.5 4.7 %collective-permute-start.13 = (f32[64,1024]{1,0:T(8,128)S(1)}, f32[64,1024]{1,0:T(8,128)S(1)}, u32[]{:S(2)}, u32[]{:S(2)}) collective-permute-start(f32[64,1024]{1,0:T(8,128)S(1)} %get-tuple-element.22), channel_id=1, source_target_pairs={{0,6},{1,7},{2,4},{3,5},{4,2},{5,3},{6,0},{7,1},{8,14},{9,15},{10,... | collective-permute-start | bytes 786440 | tf_op jit(solution)/shard_map/ppermute | solution.py:25
  84.1 0.0 collective-permute-done.10
  84.1 0.5 collective-permute-start.14
  84.6 0.0 collective-permute-done.11
  84.6 0.0 collective-permute-done.12
  84.6 4.0 %collective-permute-done.13 = f32[64,1024]{1,0:T(8,128)S(1)} collective-permute-done((f32[64,1024]{1,0:T(8,128)S(1)}, f32[64,1024]{1,0:T(8,128)S(1)}, u32[]{:S(2)}, u32[]{:S(2)}) %collective-permute-start.13) | collective-permute-done | bytes 262176 | tf_op jit(solution)/shard_map/ppermute | solution.py:25
  88.6 4.4 %collective-permute-done.14 = f32[64,1024]{1,0:T(8,128)S(1)} collective-permute-done((f32[64,1024]{1,0:T(8,128)S(1)}, f32[64,1024]{1,0:T(8,128)S(1)}, u32[]{:S(2)}, u32[]{:S(2)}) %collective-permute-start.14) | collective-permute-done | bytes 262176 | tf_op jit(solution)/shard_map/ppermute | solution.py:25
  93.0 0.0 copy-done.1
  93.0 0.0 copy-done.2
  93.0 0.2 add_add_fusion
  93.2 13.2 %collective-permute-start.16 = (f32[32,1024]{1,0:T(8,128)S(1)}, f32[32,1024]{1,0:T(8,128)S(1)}, u32[]{:S(2)}, u32[]{:S(2)}) collective-permute-start(f32[32,1024]{1,0:T(8,128)S(1)} %get-tuple-element.25), channel_id=1, source_target_pairs={{0,120},{8,0},{16,8},{24,16},{32,24},{40,32},{48,40},{56,48},{64,5... | collective-permute-start | bytes 393224 | tf_op jit(solution)/shard_map/ppermute | solution.py:20
  106.4 0.5 collective-permute-start.15
  106.9 0.0 collective-permute-done.17
  106.9 3.5 %collective-permute-done.16 = f32[32,1024]{1,0:T(8,128)S(1)} collective-permute-done((f32[32,1024]{1,0:T(8,128)S(1)}, f32[32,1024]{1,0:T(8,128)S(1)}, u32[]{:S(2)}, u32[]{:S(2)}) %collective-permute-start.16) | collective-permute-done | bytes 131104 | tf_op jit(solution)/shard_map/ppermute | solution.py:20
  110.5 0.0 collective-permute-done.15
  110.5 0.7 copy.11
  111.1 0.7 copy.12
  111.8 1.3 %copy.13 = f32[1,256,2048]{2,1,0:T(8,128)} copy(f32[1,256,2048]{2,1,0:T(8,128)S(1)} %bitcast.11) | data formatting | bytes 4194304
  (1 shorter events, 0.0 us)
Async XLA Ops:
  0.6 54.7 %collective-permute-start.7 = (f32[256,2048]{1,0:T(8,128)}, f32[256,2048]{1,0:T(8,128)}, u32[]{:S(2)}, u32[]{:S(2)}) collective-permute-start(f32[256,2048]{1,0:T(8,128)} %bitcast.19), channel_id=1, source_target_pairs={{0,64},{8,72},{16,80},{24,88},{32,96},{40,104},{48,112},{56,120},{... | collective-permute-start | bytes 6291464 | tf_op jit(solution)/shard_map/ppermute | solution.py:20
  6.1 10.8 %collective-permute-start.6 = (f32[64,1024]{1,0:T(8,128)S(1)}, f32[64,1024]{1,0:T(8,128)S(1)}, u32[]{:S(2)}, u32[]{:S(2)}) collective-permute-start(f32[64,1024]{1,0:T(8,128)S(1)} %pad_maximum_fusion.refs_1_), channel_id=1, source_target_pairs={{0,7},{1,6},{2,5},{3,4},{4,3},{5,2},{6,1},{7,0},{8,15},{9,14},{10,... | collective-permute-start | bytes 786440 | tf_op jit(solution)/shard_map/ppermute | solution.py:25
  11.4 11.5 %collective-permute-start.5 = (f32[64,1024]{1,0:T(8,128)S(1)}, f32[64,1024]{1,0:T(8,128)S(1)}, u32[]{:S(2)}, u32[]{:S(2)}) collective-permute-start(f32[64,1024]{1,0:T(8,128)S(1)} %pad_maximum_fusion.refs_1_), channel_id=1, source_target_pairs={{0,6},{1,7},{2,4},{3,5},{4,2},{5,3},{6,0},{7,1},{8,14},{9,15},{10,... | collective-permute-start | bytes 786440 | tf_op jit(solution)/shard_map/ppermute | solution.py:25
  11.7 16.5 %collective-permute-start.4 = (f32[64,1024]{1,0:T(8,128)S(1)}, f32[64,1024]{1,0:T(8,128)S(1)}, u32[]{:S(2)}, u32[]{:S(2)}) collective-permute-start(f32[64,1024]{1,0:T(8,128)S(1)} %pad_maximum_fusion.refs_1_), channel_id=1, source_target_pairs={{0,5},{1,4},{2,7},{3,6},{4,1},{5,0},{6,3},{7,2},{8,13},{9,12},{10,... | collective-permute-start | bytes 786440 | tf_op jit(solution)/shard_map/ppermute | solution.py:25
  14.3 19.7 %collective-permute-start.3 = (f32[64,1024]{1,0:T(8,128)S(1)}, f32[64,1024]{1,0:T(8,128)S(1)}, u32[]{:S(2)}, u32[]{:S(2)}) collective-permute-start(f32[64,1024]{1,0:T(8,128)S(1)} %pad_maximum_fusion.refs_1_), channel_id=1, source_target_pairs={{0,4},{1,5},{2,6},{3,7},{4,0},{5,1},{6,2},{7,3},{8,12},{9,13},{10,... | collective-permute-start | bytes 786440 | tf_op jit(solution)/shard_map/ppermute | solution.py:25
  16.9 17.1 %collective-permute-start.2 = (f32[64,1024]{1,0:T(8,128)S(1)}, f32[64,1024]{1,0:T(8,128)S(1)}, u32[]{:S(2)}, u32[]{:S(2)}) collective-permute-start(f32[64,1024]{1,0:T(8,128)S(1)} %pad_maximum_fusion.refs_1_), channel_id=1, source_target_pairs={{0,3},{1,2},{2,1},{3,0},{4,7},{5,6},{6,5},{7,4},{8,11},{9,10},{10,... | collective-permute-start | bytes 786440 | tf_op jit(solution)/shard_map/ppermute | solution.py:25
  22.9 11.7 %collective-permute-start.1 = (f32[64,1024]{1,0:T(8,128)S(1)}, f32[64,1024]{1,0:T(8,128)S(1)}, u32[]{:S(2)}, u32[]{:S(2)}) collective-permute-start(f32[64,1024]{1,0:T(8,128)S(1)} %pad_maximum_fusion.refs_1_), channel_id=1, source_target_pairs={{0,2},{1,3},{2,0},{3,1},{4,6},{5,7},{6,4},{7,5},{8,10},{9,11},{10,... | collective-permute-start | bytes 786440 | tf_op jit(solution)/shard_map/ppermute | solution.py:25
  28.2 11.7 %collective-permute-start = (f32[64,1024]{1,0:T(8,128)S(1)}, f32[64,1024]{1,0:T(8,128)S(1)}, u32[]{:S(2)}, u32[]{:S(2)}) collective-permute-start(f32[64,1024]{1,0:T(8,128)S(1)} %pad_maximum_fusion.refs_1_), channel_id=1, source_target_pairs={{0,1},{1,0},{2,3},{3,2},{4,5},{5,4},{6,7},{7,6},{8,9},{9,8},{10,11... | collective-permute-start | bytes 786440 | tf_op jit(solution)/shard_map/ppermute | solution.py:25
  55.0 51.9 %collective-permute-start.17 = (f32[256,2048]{1,0:T(8,128)S(1)}, f32[256,2048]{1,0:T(8,128)S(1)}, u32[]{:S(2)}, u32[]{:S(2)}) collective-permute-start(f32[256,2048]{1,0:T(8,128)S(1)} %get-tuple-element.24), channel_id=1, source_target_pairs={{0,64},{8,72},{16,80},{24,88},{32,96},{40,104},{48,112},{56,120},{... | collective-permute-start | bytes 6291464 | tf_op jit(solution)/shard_map/ppermute | solution.py:20
  55.4 1.6 %copy-start = (f32[256,2048]{1,0:T(8,128)S(1)}, f32[256,2048]{1,0:T(8,128)}, u32[]{:S(2)}) copy-start(f32[256,2048]{1,0:T(8,128)} %get-tuple-element.14.refs_1_) | copy-start | bytes 6291460
  56.9 36.0 %copy-start.1 = (f32[1,32,1024]{2,1,0:T(8,128)S(1)}, f32[1,32,1024]{2,1,0:T(8,128)}, u32[]{:S(2)}) copy-start(f32[1,32,1024]{2,1,0:T(8,128)} %param.6) | copy-start | bytes 393220
  56.9 36.0 %copy-start.2 = (f32[1,32,1024]{2,1,0:T(8,128)S(1)}, f32[1,32,1024]{2,1,0:T(8,128)}, u32[]{:S(2)}) copy-start(f32[1,32,1024]{2,1,0:T(8,128)} %param.5) | copy-start | bytes 393220
  66.3 6.7 %collective-permute-start.8 = (f32[64,1024]{1,0:T(8,128)S(1)}, f32[64,1024]{1,0:T(8,128)S(1)}, u32[]{:S(2)}, u32[]{:S(2)}) collective-permute-start(f32[64,1024]{1,0:T(8,128)S(1)} %get-tuple-element.17), channel_id=1, source_target_pairs={{0,1},{1,0},{2,3},{3,2},{4,5},{5,4},{6,7},{7,6},{8,9},{9,8},{10,11... | collective-permute-start | bytes 786440 | tf_op jit(solution)/shard_map/ppermute | solution.py:25
  67.6 11.9 %collective-permute-start.9 = (f32[64,1024]{1,0:T(8,128)S(1)}, f32[64,1024]{1,0:T(8,128)S(1)}, u32[]{:S(2)}, u32[]{:S(2)}) collective-permute-start(f32[64,1024]{1,0:T(8,128)S(1)} %get-tuple-element.18), channel_id=1, source_target_pairs={{0,2},{1,3},{2,0},{3,1},{4,6},{5,7},{6,4},{7,5},{8,10},{9,11},{10,... | collective-permute-start | bytes 786440 | tf_op jit(solution)/shard_map/ppermute | solution.py:25
  68.3 15.9 %collective-permute-start.10 = (f32[64,1024]{1,0:T(8,128)S(1)}, f32[64,1024]{1,0:T(8,128)S(1)}, u32[]{:S(2)}, u32[]{:S(2)}) collective-permute-start(f32[64,1024]{1,0:T(8,128)S(1)} %get-tuple-element.19), channel_id=1, source_target_pairs={{0,3},{1,2},{2,1},{3,0},{4,7},{5,6},{6,5},{7,4},{8,11},{9,10},{10,... | collective-permute-start | bytes 786440 | tf_op jit(solution)/shard_map/ppermute | solution.py:25
  70.3 14.4 %collective-permute-start.11 = (f32[64,1024]{1,0:T(8,128)S(1)}, f32[64,1024]{1,0:T(8,128)S(1)}, u32[]{:S(2)}, u32[]{:S(2)}) collective-permute-start(f32[64,1024]{1,0:T(8,128)S(1)} %get-tuple-element.20), channel_id=1, source_target_pairs={{0,4},{1,5},{2,6},{3,7},{4,0},{5,1},{6,2},{7,3},{8,12},{9,13},{10,... | collective-permute-start | bytes 786440 | tf_op jit(solution)/shard_map/ppermute | solution.py:25
  73.0 11.6 %collective-permute-start.12 = (f32[64,1024]{1,0:T(8,128)S(1)}, f32[64,1024]{1,0:T(8,128)S(1)}, u32[]{:S(2)}, u32[]{:S(2)}) collective-permute-start(f32[64,1024]{1,0:T(8,128)S(1)} %get-tuple-element.21), channel_id=1, source_target_pairs={{0,5},{1,4},{2,7},{3,6},{4,1},{5,0},{6,3},{7,2},{8,13},{9,12},{10,... | collective-permute-start | bytes 786440 | tf_op jit(solution)/shard_map/ppermute | solution.py:25
  79.5 9.1 %collective-permute-start.13 = (f32[64,1024]{1,0:T(8,128)S(1)}, f32[64,1024]{1,0:T(8,128)S(1)}, u32[]{:S(2)}, u32[]{:S(2)}) collective-permute-start(f32[64,1024]{1,0:T(8,128)S(1)} %get-tuple-element.22), channel_id=1, source_target_pairs={{0,6},{1,7},{2,4},{3,5},{4,2},{5,3},{6,0},{7,1},{8,14},{9,15},{10,... | collective-permute-start | bytes 786440 | tf_op jit(solution)/shard_map/ppermute | solution.py:25
  84.1 8.8 %collective-permute-start.14 = (f32[64,1024]{1,0:T(8,128)S(1)}, f32[64,1024]{1,0:T(8,128)S(1)}, u32[]{:S(2)}, u32[]{:S(2)}) collective-permute-start(f32[64,1024]{1,0:T(8,128)S(1)} %get-tuple-element.23), channel_id=1, source_target_pairs={{0,7},{1,6},{2,5},{3,4},{4,3},{5,2},{6,1},{7,0},{8,15},{9,14},{10,... | collective-permute-start | bytes 786440 | tf_op jit(solution)/shard_map/ppermute | solution.py:25
  93.2 17.3 %collective-permute-start.16 = (f32[32,1024]{1,0:T(8,128)S(1)}, f32[32,1024]{1,0:T(8,128)S(1)}, u32[]{:S(2)}, u32[]{:S(2)}) collective-permute-start(f32[32,1024]{1,0:T(8,128)S(1)} %get-tuple-element.25), channel_id=1, source_target_pairs={{0,120},{8,0},{16,8},{24,16},{32,24},{40,32},{48,40},{56,48},{64,5... | collective-permute-start | bytes 393224 | tf_op jit(solution)/shard_map/ppermute | solution.py:20
  106.4 4.1 %collective-permute-start.15 = (f32[32,1024]{1,0:T(8,128)S(1)}, f32[32,1024]{1,0:T(8,128)S(1)}, u32[]{:S(2)}, u32[]{:S(2)}) collective-permute-start(f32[32,1024]{1,0:T(8,128)S(1)} %get-tuple-element.26), channel_id=1, source_target_pairs={{0,8},{8,16},{16,24},{24,32},{32,40},{40,48},{48,56},{56,64},{64,7... | collective-permute-start | bytes 393224 | tf_op jit(solution)/shard_map/ppermute | solution.py:20

commit v2 on v0

v2 whole, which is shorter than its diff:
```python
import functools
import math

import jax
import jax.numpy as jnp
from jax import lax
from jax.experimental import pallas as pl
from jax.experimental.pallas import tpu as pltpu
from jax.sharding import PartitionSpec as P

F32 = jnp.float32
BF16 = jnp.bfloat16
ROOT_HALF = math.sqrt(0.5)
DENSITY = 1.0 / math.sqrt(2.0 * math.pi)
COST = {"pre": 10**3, "dact": 10**3, "out": 10**3, "back": 10**12}
VMEM_LIMIT = 48 * 1024 * 1024


def shifted(value, by):
    length = lax.axis_size("section")
    return lax.ppermute(value, "section", [(i, (i + by) % length) for i in range(length)])


def across(value, mask):
    length = lax.axis_size("tensor")
    return lax.ppermute(value, "tensor", [(i, i ^ mask) for i in range(length)])


def halves(value):
    high = value.astype(BF16)
    return high, (value - high.astype(F32)).astype(BF16)


def product(left, right, contract):
    dims = (contract, ((), ()))
    (lh, ll), (rh, rl) = left, right
    dot = functools.partial(lax.dot_general, dimension_numbers=dims, preferred_element_type=F32)
    return dot(lh, rh) + (dot(lh, rl) + dot(ll, rh))


PLAIN = ((1,), (0,))
TURNED = ((1,), (1,))


def gelu(value):
    return 0.5 * value * (1.0 + lax.erf(value * ROOT_HALF))


def gelu_slope(value):
    return 0.5 * (1.0 + lax.erf(value * ROOT_HALF)) + value * (jnp.exp(-0.5 * value * value) * DENSITY)


def assemble(place_ref, pairs, high_ref, low_ref):
    rows = pairs[0].shape[0] // 2
    for mask in range(2 * len(pairs)):
        at = pl.ds(pl.multiple_of((place_ref[0] ^ mask) * rows, rows), rows)
        start = mask // len(pairs) * rows
        high_ref[at, :], low_ref[at, :] = halves(pairs[mask % len(pairs)][start : start + rows])


def in_kernel(contract, place_ref, *refs):
    *pairs, weight_ref, result_ref, high, low = refs

    @pl.when(pl.program_id(0) == 0)
    def _():
        assemble(place_ref, pairs, high, low)

    result_ref[...] = product((high[...], low[...]), halves(weight_ref[...]), contract)


def out_kernel(pre_ref, second_ref, sum_ref):
    @pl.when(pl.program_id(0) == 0)
    def _():
        sum_ref[...] = jnp.zeros_like(sum_ref)

    sum_ref[...] += product(halves(gelu(pre_ref[...])), halves(second_ref[...]), PLAIN)


def back_kernel(dact_ref, old_ref, first_ref, sum_ref):
    @pl.when(pl.program_id(0) == 0)
    def _():
        sum_ref[...] = jnp.zeros_like(sum_ref)

    hidden_grad = dact_ref[...] * gelu_slope(old_ref[...])
    sum_ref[...] += product(halves(hidden_grad), halves(first_ref[...]), TURNED)


def kernel_call(body, name, tile, inputs, kinds, outputs, scratch, products=1):
    def spec(shape, kind):
        if kind == "scalar":
            return pl.BlockSpec(memory_space=pltpu.SMEM)
        if kind == "column":
            return pl.BlockSpec((shape[0], tile), lambda j: (0, j))
        if kind == "row":
            return pl.BlockSpec((tile, shape[1]), lambda j: (j, 0))
        return pl.BlockSpec(shape, lambda j: (0, 0))

    shapes = [value.shape for value in inputs]
    hidden, depth = max(shapes[-1]), min(shapes[-1])
    rows = outputs[0][0][0]
    moved = sum(4 * math.prod(shape) for shape in shapes + [shape for shape, _ in outputs])
    return pl.pallas_call(
        body,
        grid=(hidden // tile,),
        out_shape=[jax.ShapeDtypeStruct(shape, F32) for shape, _ in outputs],
        in_specs=[spec(shape, kind) for shape, kind in zip(shapes, kinds)],
        out_specs=[spec(shape, kind) for shape, kind in outputs],
        scratch_shapes=scratch,
        compiler_params=pltpu.CompilerParams(
            dimension_semantics=("arbitrary",), vmem_limit_bytes=VMEM_LIMIT
        ),
        cost_estimate=pl.CostEstimate(
            flops=COST[name], bytes_accessed=1000, transcendentals=0
        ),
        name=name,
    )(*inputs)


def exchanged(value):
    return lax.all_to_all(value, "tensor", 0, 0, tiled=True)


def scattered(rows, value):
    return rows + jnp.sum(exchanged(value).reshape(-1, *rows.shape), axis=0)


def shards(fwd_input, out_grad, w_inner, w_outer, lent_saved):
    half = lax.axis_size("section") // 2
    parts = lax.axis_size("tensor")
    place = lax.axis_index("tensor").astype(jnp.int32)[None]
    x_rows, g_rows, w_first, w_second = fwd_input[0], out_grad[0], w_inner[0], w_outer[0]

    old_pre = shifted(lent_saved[0], half)
    total, depth = parts * x_rows.shape[0], x_rows.shape[1]
    wide, narrow = (total, w_first.shape[1]), (total, depth)
    scratch = [pltpu.VMEM(narrow, BF16)] * 2

    def gathered(rows):
        pair = jnp.concatenate([rows, across(rows, parts // 2)])
        return [pair] + [across(pair, mask) for mask in range(1, parts // 2)]

    x_pairs, g_pairs = gathered(x_rows), gathered(g_rows)
    kinds = ["scalar"] + [""] * len(x_pairs)
    (pre,) = kernel_call(
        functools.partial(in_kernel, PLAIN), "pre", 512, [place, *x_pairs, w_first], kinds + ["column"],
        [(wide, "column")], scratch,
    )
    given = shifted(pre, half)
    (d_act,) = kernel_call(
        functools.partial(in_kernel, TURNED), "dact", 512, [place, *g_pairs, w_second], kinds + ["row"],
        [(wide, "column")], scratch,
    )
    (fwd_sum,) = kernel_call(out_kernel, "out", 512, [pre, w_second], ["column", "row"], [(narrow, "")], [])
    moved_out = shifted(scattered(x_rows, fwd_sum), 1)
    (bwd_sum,) = kernel_call(
        back_kernel, "back", 512, [d_act, old_pre, w_first], ["column", "column", "column"], [(narrow, "")], []
    )
    moved_grad = shifted(scattered(g_rows, bwd_sum), -1)
    return (moved_out[None], moved_grad[None], given[None])


def solution(mesh):
    return jax.shard_map(
        shards,
        mesh=mesh,
        in_specs=(
            P("section", "tensor", None),
            P("section", "tensor", None),
            P("section", None, "tensor"),
            P("section", "tensor", None),
            P("section", None, "tensor"),
        ),
        out_specs=(
            P("section", "tensor", None),
            P("section", "tensor", None),
            P("section", None, "tensor"),
        ),
        check_vma=False,
    )
```

time: 272 us -> 103 us (0.38)
  waiting for transfers between devices: 198 us -> 21.8 us
  matrix products: 41.1 us -> 0 us
  Pallas kernels: 0 us -> 30.2 us
  starting transfers between devices: 12.8 us -> 41.2 us
  between operations: 13.8 us -> 0.73 us
    reduce_scatter x2 -> x0, waiting for transfers between devices: 120 us -> none  [the longest x1 70.6 us: backward_pass(): lax.psum_scatter(lax.dot_general(d_pre, w_first, (((1,), (1,)), ((), ()))...]
    all_gather x2 -> x0, waiting for transfers between devices: 73.9 us -> none  [the longest x1 45.3 us: forward_pass(): lax.all_gather(x_rows, 'tensor', axis=0, tiled=True)]
    dot_general x4 -> x0, matrix products: 41.1 us -> none  [the longest x1 12.7 us: backward_pass(): lax.dot_general(d_pre, w_first, (((1,), (1,)), ((), ())), precision=lax.P...]
    pallas_call x0 -> x4, Pallas kernels: none -> 30.2 us  [kernel_call(): pl.pallas_call(body, grid=(hidden // tile,), out_shape=[jax.ShapeDtypeStr...]
    ppermute x4 -> x12, starting transfers between devices: 12.5 us -> 30 us  [the longest x8 15 us: across(): return lax.ppermute(value, 'tensor', [(i, i ^ mask) for i in range(length)])]
    ppermute x4 -> x12, waiting for transfers between devices: 3.02 us -> 15.2 us  [the longest x8 8.07 us: across(): return lax.ppermute(value, 'tensor', [(i, i ^ mask) for i in range(length)])]
    all_to_all x0 -> x2, starting transfers between devices: none -> 11.2 us  [exchanged(): return lax.all_to_all(value, 'tensor', 0, 0, tiled=True)]
    all_to_all x0 -> x2, waiting for transfers between devices: none -> 6.6 us  [exchanged(): return lax.all_to_all(value, 'tensor', 0, 0, tiled=True)]
  transfers between devices with their start and end apart: 8 -> 14, of which waited for: 5 -> 5; matrix products, arithmetic and copies ran while one was open for 16% -> 3% of each run, Pallas kernels for 0% -> 30%
where the time goes in v2:
time: 103 us; the launch traced here: 102 us
  starting transfers between devices  41.2 us (40%)
  Pallas kernels  30.2 us (29%)
  waiting for transfers between devices  21.8 us (21%)
  local copies, waits for them, and re-layouts  4.45 us (4%)
  other arithmetic  3.23 us (3%)
    pallas_call x4, Pallas kernels, kernel_call(): pl.pallas_call(body, grid=(hidden // tile,), out_shape=[jax.ShapeDtypeStr...  30.2 us
    ppermute x8, starting transfers between devices, across(): return lax.ppermute(value, 'tensor', [(i, i ^ mask) for i in range(length)])  15 us
    ppermute x4, starting transfers between devices, shifted(): lax.ppermute(value, 'section', [(i, (i + by) % length) for i in range(len...  14.9 us
    all_to_all x2, starting transfers between devices, exchanged(): return lax.all_to_all(value, 'tensor', 0, 0, tiled=True)  11.2 us
    ppermute x8, waiting for transfers between devices, across(): return lax.ppermute(value, 'tensor', [(i, i ^ mask) for i in range(length)])  8.07 us
    ppermute x4, waiting for transfers between devices, shifted(): lax.ppermute(value, 'section', [(i, (i + by) % length) for i in range(len...  7.11 us
    all_to_all x2, waiting for transfers between devices, exchanged(): return lax.all_to_all(value, 'tensor', 0, 0, tiled=True)  6.6 us
    unnamed x7, local copies, waits for them, and re-layouts  4.45 us
  transfers between devices with their start and end apart: 14, of which 5 were waited for; matrix products, arithmetic and copies ran while one was open for 3% of the time, Pallas kernels for 30%

profile of v2, /device:TPU:1, one launch (start us, length us, event | category | flops | bytes accessed | tf_op | source)
XLA Modules:
  0.0 101.6 jit_solution(14796026625484819255)
XLA Ops:
  0.6 4.5 %collective-permute-start.9 = (f32[256,2048]{1,0:T(8,128)}, f32[256,2048]{1,0:T(8,128)}, u32[]{:S(2)}, u32[]{:S(2)}) collective-permute-start(f32[256,2048]{1,0:T(8,128)} %bitcast.23), channel_id=1, source_target_pairs={{0,64},{8,72},{16,80},{24,88},{32,96},{40,104},{48,112},{56,120},{... | collective-permute-start | bytes 6291464 | tf_op jit(solution)/shard_map/ppermute | solution.py:21
  5.1 2.7 %collective-permute-start = (f32[32,1024]{1,0:T(8,128)}, f32[32,1024]{1,0:T(8,128)S(1)}, u32[]{:S(2)}, u32[]{:S(2)}) collective-permute-start(f32[32,1024]{1,0:T(8,128)} %bitcast.17), channel_id=1, source_target_pairs={{0,4},{1,5},{2,6},{3,7},{4,0},{5,1},{6,2},{7,3},{8,12},{9,13},{10,... | collective-permute-start | bytes 393224 | tf_op jit(solution)/shard_map/ppermute | solution.py:26
  7.9 3.2 %collective-permute-done = f32[32,1024]{1,0:T(8,128)S(1)} collective-permute-done((f32[32,1024]{1,0:T(8,128)}, f32[32,1024]{1,0:T(8,128)S(1)}, u32[]{:S(2)}, u32[]{:S(2)}) %collective-permute-start) | collective-permute-done | bytes 131104 | tf_op jit(solution)/shard_map/ppermute | solution.py:26
  11.1 0.9 pad_maximum_fusion.refs_0_
  12.0 2.8 %collective-permute-start.3 = (f32[64,1024]{1,0:T(8,128)S(1)}, f32[64,1024]{1,0:T(8,128)S(1)}, u32[]{:S(2)}, u32[]{:S(2)}) collective-permute-start(f32[64,1024]{1,0:T(8,128)S(1)} %pad_maximum_fusion.refs_0_), channel_id=1, source_target_pairs={{0,3},{1,2},{2,1},{3,0},{4,7},{5,6},{6,5},{7,4},{8,11},{9,10},{10,... | collective-permute-start | bytes 786440 | tf_op jit(solution)/shard_map/ppermute | solution.py:26
  14.8 0.3 collective-permute-start.2
  15.2 2.7 %collective-permute-start.5 = (f32[32,1024]{1,0:T(8,128)}, f32[32,1024]{1,0:T(8,128)S(1)}, u32[]{:S(2)}, u32[]{:S(2)}) collective-permute-start(f32[32,1024]{1,0:T(8,128)} %bitcast.19), channel_id=1, source_target_pairs={{0,4},{1,5},{2,6},{3,7},{4,0},{5,1},{6,2},{7,3},{8,12},{9,13},{10,... | collective-permute-start | bytes 393224 | tf_op jit(solution)/shard_map/ppermute | solution.py:26
  17.9 0.3 collective-permute-start.1
  18.2 2.9 %collective-permute-done.5 = f32[32,1024]{1,0:T(8,128)S(1)} collective-permute-done((f32[32,1024]{1,0:T(8,128)}, f32[32,1024]{1,0:T(8,128)S(1)}, u32[]{:S(2)}, u32[]{:S(2)}) %collective-permute-start.5) | collective-permute-done | bytes 131104 | tf_op jit(solution)/shard_map/ppermute | solution.py:26
  21.1 0.9 pad_maximum_fusion.1.refs_0_
  22.0 2.0 %collective-permute-start.8 = (f32[64,1024]{1,0:T(8,128)S(1)}, f32[64,1024]{1,0:T(8,128)S(1)}, u32[]{:S(2)}, u32[]{:S(2)}) collective-permute-start(f32[64,1024]{1,0:T(8,128)S(1)} %pad_maximum_fusion.1.refs_0_), channel_id=1, source_target_pairs={{0,3},{1,2},{2,1},{3,0},{4,7},{5,6},{6,5},{7,4},{8,11},{9,10},{10,... | collective-permute-start | bytes 786440 | tf_op jit(solution)/shard_map/ppermute | solution.py:26
  24.0 2.0 %collective-permute-done.3.refs_3_ = f32[64,1024]{1,0:T(8,128)S(1)} collective-permute-done((f32[64,1024]{1,0:T(8,128)S(1)}, f32[64,1024]{1,0:T(8,128)S(1)}, u32[]{:S(2)}, u32[]{:S(2)}) %collective-permute-start.3) | collective-permute-done | bytes 262176 | tf_op jit(solution)/shard_map/ppermute | solution.py:26
  26.0 0.8 collective-permute-start.7
  26.8 0.0 collective-permute-done.2.refs_2_
  26.8 3.3 %collective-permute-start.6 = (f32[64,1024]{1,0:T(8,128)S(1)}, f32[64,1024]{1,0:T(8,128)S(1)}, u32[]{:S(2)}, u32[]{:S(2)}) collective-permute-start(f32[64,1024]{1,0:T(8,128)S(1)} %pad_maximum_fusion.1.refs_0_), channel_id=1, source_target_pairs={{0,1},{1,0},{2,3},{3,2},{4,5},{5,4},{6,7},{7,6},{8,9},{9,8},{10,11... | collective-permute-start | bytes 786440 | tf_op jit(solution)/shard_map/ppermute | solution.py:26
  30.1 0.0 collective-permute-done.1.refs_1_
  30.1 7.4 %pre.1.pre_ref = f32[256,2048]{1,0:T(8,128)} custom-call(s32[1]{0:T(128)} %bitcast.1.place_ref, f32[64,1024]{1,0:T(8,128)S(1)} %pad_maximum_fusion.refs_0_, f32[64,1024]{1,0:T(8,128)S(1)} %collective-permute-done.1.refs_1_, f32[64,1024]{1,0:T(8,128)S(1)} %collective-permute-done.2.refs_2_, f32[64,1024]{1,0:T(8,128)S(1)} %collective-permute-done.3.refs_3_, ...), custom_call_target="tpu_custom_call" | custom-call | flops 1000 | bytes 1000 | tf_op jit(solution)/shard_map/pre/pallas_call | solution.py:102
  37.5 0.1 collective-permute-start.11
  37.7 7.8 %out.1 = f32[256,1024]{1,0:T(8,128)} custom-call(f32[256,2048]{1,0:T(8,128)} %pre.1.pre_ref, f32[2048,1024]{1,0:T(8,128)} %bitcast.13), custom_call_target="tpu_custom_call" | custom-call | flops 1000 | bytes 1000 | tf_op jit(solution)/shard_map/out/pallas_call | solution.py:102
  45.5 4.5 %all-to-all-start = ((f32[8,32,1024]{2,1,0:T(8,128)}), f32[8,32,1024]{2,1,0:T(8,128)}, u32[]{:S(2)}, u32[]{:S(2)}) async-start(f32[8,32,1024]{2,1,0:T(8,128)} %bitcast.4), calls=%async_computation | async-start | bytes 2097152 | tf_op jit(solution)/shard_map/all_to_all | solution.py:120
  50.0 0.0 collective-permute-done.8.refs_3_
  50.0 0.0 collective-permute-done.7.refs_2_
  50.0 0.0 collective-permute-done.6.refs_1_
  50.0 6.6 %dact.1.dact_ref = f32[256,2048]{1,0:T(8,128)S(1)} custom-call(s32[1]{0:T(128)} %bitcast.1.place_ref, f32[64,1024]{1,0:T(8,128)S(1)} %pad_maximum_fusion.1.refs_0_, f32[64,1024]{1,0:T(8,128)S(1)} %collective-permute-done.6.refs_1_, f32[64,1024]{1,0:T(8,128)S(1)} %collective-permute-done.7.refs_2_, f32[64,1024]{1,0:T(8,128)S(1)} %collective-permute-done.8.refs_3_, ...), custom_call_target="tpu_custom_call" | custom-call | flops 1000 | bytes 1000 | tf_op jit(solution)/shard_map/dact/pallas_call | solution.py:102
  56.6 0.0 collective-permute-done.9.old_ref
  56.6 8.3 %back.1 = f32[256,1024]{1,0:T(8,128)} custom-call(f32[256,2048]{1,0:T(8,128)S(1)} %dact.1.dact_ref, f32[256,2048]{1,0:T(8,128)} %collective-permute-done.9.old_ref, f32[1024,2048]{1,0:T(8,128)} %bitcast.16), custom_call_target="tpu_custom_call" | custom-call | flops 999999995904 | bytes 1000 | tf_op jit(solution)/shard_map/back/pallas_call | solution.py:102
  64.9 0.0 copy-start
  64.9 0.0 all-to-all-done
  64.9 0.0 copy-start.1
  64.9 6.8 %all-to-all-start.1 = ((f32[8,32,1024]{2,1,0:T(8,128)}), f32[8,32,1024]{2,1,0:T(8,128)S(1)}, u32[]{:S(2)}, u32[]{:S(2)}) async-start(f32[8,32,1024]{2,1,0:T(8,128)} %bitcast.8), calls=%async_computation.1 | async-start | bytes 2097152 | tf_op jit(solution)/shard_map/all_to_all | solution.py:120
  71.7 1.3 %reduce_sum.18 = f32[32,1024]{1,0:T(8,128)S(1)} reduce(f32[8,32,1024]{2,1,0:T(8,128)} %all-to-all-done, f32[]{:T(128)} %constant.1.clone.1), dimensions={0}, to_apply=%region_0.0 | reduce | flops 229376 | bytes 1179652 | tf_op jit(solution)/shard_map/reduce_sum | solution.py:124
  73.0 0.0 copy-done
  73.1 3.9 %collective-permute-start.4 = (f32[32,1024]{1,0:T(8,128)S(1)}, f32[32,1024]{1,0:T(8,128)S(1)}, u32[]{:S(2)}, u32[]{:S(2)}) collective-permute-start(f32[32,1024]{1,0:T(8,128)S(1)} %bitcast_add_fusion.1), channel_id=1, source_target_pairs={{0,8},{8,16},{16,24},{24,32},{32,40},{40,48},{48,56},{56,64},{64,7... | collective-permute-start | bytes 393224 | tf_op jit(solution)/shard_map/ppermute | solution.py:21
  76.9 6.6 %all-to-all-done.1 = f32[8,32,1024]{2,1,0:T(8,128)S(1)} async-done(((f32[8,32,1024]{2,1,0:T(8,128)}), f32[8,32,1024]{2,1,0:T(8,128)S(1)}, u32[]{:S(2)}, u32[]{:S(2)}) %all-to-all-start.1) | async-done | bytes 1048608 | tf_op jit(solution)/shard_map/all_to_all | solution.py:120
  83.5 0.1 reduce_sum.19
  83.6 0.0 copy-done.1
  83.6 6.4 %collective-permute-start.10 = (f32[32,1024]{1,0:T(8,128)S(1)}, f32[32,1024]{1,0:T(8,128)S(1)}, u32[]{:S(2)}, u32[]{:S(2)}) collective-permute-start(f32[32,1024]{1,0:T(8,128)S(1)} %bitcast_add_fusion), channel_id=1, source_target_pairs={{0,120},{8,0},{16,8},{24,16},{32,24},{40,32},{48,40},{56,48},{64,5... | collective-permute-start | bytes 393224 | tf_op jit(solution)/shard_map/ppermute | solution.py:21
  90.1 0.0 collective-permute-done.4
  90.1 7.1 %collective-permute-done.11 = f32[256,2048]{1,0:T(8,128)} collective-permute-done((f32[256,2048]{1,0:T(8,128)}, f32[256,2048]{1,0:T(8,128)}, u32[]{:S(2)}, u32[]{:S(2)}) %collective-permute-start.11) | collective-permute-done | bytes 2097184 | tf_op jit(solution)/shard_map/ppermute | solution.py:21
  97.2 0.0 collective-permute-done.10
  97.2 0.7 copy.11
  97.8 0.7 copy.12
  98.5 3.1 %copy.13 = f32[1,256,2048]{2,1,0:T(8,128)} copy(f32[1,256,2048]{2,1,0:T(8,128)} %bitcast.10) | data formatting | bytes 4194304
  (2 shorter events, 0.0 us)
Async XLA Ops:
  0.6 56.0 %collective-permute-start.9 = (f32[256,2048]{1,0:T(8,128)}, f32[256,2048]{1,0:T(8,128)}, u32[]{:S(2)}, u32[]{:S(2)}) collective-permute-start(f32[256,2048]{1,0:T(8,128)} %bitcast.23), channel_id=1, source_target_pairs={{0,64},{8,72},{16,80},{24,88},{32,96},{40,104},{48,112},{56,120},{... | collective-permute-start | bytes 6291464 | tf_op jit(solution)/shard_map/ppermute | solution.py:21
  5.1 5.9 %collective-permute-start = (f32[32,1024]{1,0:T(8,128)}, f32[32,1024]{1,0:T(8,128)S(1)}, u32[]{:S(2)}, u32[]{:S(2)}) collective-permute-start(f32[32,1024]{1,0:T(8,128)} %bitcast.17), channel_id=1, source_target_pairs={{0,4},{1,5},{2,6},{3,7},{4,0},{5,1},{6,2},{7,3},{8,12},{9,13},{10,... | collective-permute-start | bytes 393224 | tf_op jit(solution)/shard_map/ppermute | solution.py:26
  12.0 14.0 %collective-permute-start.3 = (f32[64,1024]{1,0:T(8,128)S(1)}, f32[64,1024]{1,0:T(8,128)S(1)}, u32[]{:S(2)}, u32[]{:S(2)}) collective-permute-start(f32[64,1024]{1,0:T(8,128)S(1)} %pad_maximum_fusion.refs_0_), channel_id=1, source_target_pairs={{0,3},{1,2},{2,1},{3,0},{4,7},{5,6},{6,5},{7,4},{8,11},{9,10},{10,... | collective-permute-start | bytes 786440 | tf_op jit(solution)/shard_map/ppermute | solution.py:26
  14.8 12.0 %collective-permute-start.2 = (f32[64,1024]{1,0:T(8,128)S(1)}, f32[64,1024]{1,0:T(8,128)S(1)}, u32[]{:S(2)}, u32[]{:S(2)}) collective-permute-start(f32[64,1024]{1,0:T(8,128)S(1)} %pad_maximum_fusion.refs_0_), channel_id=1, source_target_pairs={{0,2},{1,3},{2,0},{3,1},{4,6},{5,7},{6,4},{7,5},{8,10},{9,11},{10,... | collective-permute-start | bytes 786440 | tf_op jit(solution)/shard_map/ppermute | solution.py:26
  15.2 5.9 %collective-permute-start.5 = (f32[32,1024]{1,0:T(8,128)}, f32[32,1024]{1,0:T(8,128)S(1)}, u32[]{:S(2)}, u32[]{:S(2)}) collective-permute-start(f32[32,1024]{1,0:T(8,128)} %bitcast.19), channel_id=1, source_target_pairs={{0,4},{1,5},{2,6},{3,7},{4,0},{5,1},{6,2},{7,3},{8,12},{9,13},{10,... | collective-permute-start | bytes 393224 | tf_op jit(solution)/shard_map/ppermute | solution.py:26
  17.9 12.2 %collective-permute-start.1 = (f32[64,1024]{1,0:T(8,128)S(1)}, f32[64,1024]{1,0:T(8,128)S(1)}, u32[]{:S(2)}, u32[]{:S(2)}) collective-permute-start(f32[64,1024]{1,0:T(8,128)S(1)} %pad_maximum_fusion.refs_0_), channel_id=1, source_target_pairs={{0,1},{1,0},{2,3},{3,2},{4,5},{5,4},{6,7},{7,6},{8,9},{9,8},{10,11... | collective-permute-start | bytes 786440 | tf_op jit(solution)/shard_map/ppermute | solution.py:26
  22.0 27.9 %collective-permute-start.8 = (f32[64,1024]{1,0:T(8,128)S(1)}, f32[64,1024]{1,0:T(8,128)S(1)}, u32[]{:S(2)}, u32[]{:S(2)}) collective-permute-start(f32[64,1024]{1,0:T(8,128)S(1)} %pad_maximum_fusion.1.refs_0_), channel_id=1, source_target_pairs={{0,3},{1,2},{2,1},{3,0},{4,7},{5,6},{6,5},{7,4},{8,11},{9,10},{10,... | collective-permute-start | bytes 786440 | tf_op jit(solution)/shard_map/ppermute | solution.py:26
  26.0 24.0 %collective-permute-start.7 = (f32[64,1024]{1,0:T(8,128)S(1)}, f32[64,1024]{1,0:T(8,128)S(1)}, u32[]{:S(2)}, u32[]{:S(2)}) collective-permute-start(f32[64,1024]{1,0:T(8,128)S(1)} %pad_maximum_fusion.1.refs_0_), channel_id=1, source_target_pairs={{0,2},{1,3},{2,0},{3,1},{4,6},{5,7},{6,4},{7,5},{8,10},{9,11},{10,... | collective-permute-start | bytes 786440 | tf_op jit(solution)/shard_map/ppermute | solution.py:26
  26.8 23.2 %collective-permute-start.6 = (f32[64,1024]{1,0:T(8,128)S(1)}, f32[64,1024]{1,0:T(8,128)S(1)}, u32[]{:S(2)}, u32[]{:S(2)}) collective-permute-start(f32[64,1024]{1,0:T(8,128)S(1)} %pad_maximum_fusion.1.refs_0_), channel_id=1, source_target_pairs={{0,1},{1,0},{2,3},{3,2},{4,5},{5,4},{6,7},{7,6},{8,9},{9,8},{10,11... | collective-permute-start | bytes 786440 | tf_op jit(solution)/shard_map/ppermute | solution.py:26
  37.5 59.6 %collective-permute-start.11 = (f32[256,2048]{1,0:T(8,128)}, f32[256,2048]{1,0:T(8,128)}, u32[]{:S(2)}, u32[]{:S(2)}) collective-permute-start(f32[256,2048]{1,0:T(8,128)} %pre.1.pre_ref), channel_id=1, source_target_pairs={{0,64},{8,72},{16,80},{24,88},{32,96},{40,104},{48,112},{56,120},{... | collective-permute-start | bytes 6291464 | tf_op jit(solution)/shard_map/ppermute | solution.py:21
  45.5 19.4 %all-to-all-start = ((f32[8,32,1024]{2,1,0:T(8,128)}), f32[8,32,1024]{2,1,0:T(8,128)}, u32[]{:S(2)}, u32[]{:S(2)}) async-start(f32[8,32,1024]{2,1,0:T(8,128)} %bitcast.4), calls=%async_computation | async-start | bytes 2097152 | tf_op jit(solution)/shard_map/all_to_all | solution.py:120
  64.9 8.1 %copy-start = (f32[1,32,1024]{2,1,0:T(8,128)S(1)}, f32[1,32,1024]{2,1,0:T(8,128)}, u32[]{:S(2)}) copy-start(f32[1,32,1024]{2,1,0:T(8,128)} %param.5) | copy-start | bytes 393220
  64.9 18.7 %copy-start.1 = (f32[1,32,1024]{2,1,0:T(8,128)S(1)}, f32[1,32,1024]{2,1,0:T(8,128)}, u32[]{:S(2)}) copy-start(f32[1,32,1024]{2,1,0:T(8,128)} %param.6) | copy-start | bytes 393220
  64.9 18.6 %all-to-all-start.1 = ((f32[8,32,1024]{2,1,0:T(8,128)}), f32[8,32,1024]{2,1,0:T(8,128)S(1)}, u32[]{:S(2)}, u32[]{:S(2)}) async-start(f32[8,32,1024]{2,1,0:T(8,128)} %bitcast.8), calls=%async_computation.1 | async-start | bytes 2097152 | tf_op jit(solution)/shard_map/all_to_all | solution.py:120
  73.1 17.0 %collective-permute-start.4 = (f32[32,1024]{1,0:T(8,128)S(1)}, f32[32,1024]{1,0:T(8,128)S(1)}, u32[]{:S(2)}, u32[]{:S(2)}) collective-permute-start(f32[32,1024]{1,0:T(8,128)S(1)} %bitcast_add_fusion.1), channel_id=1, source_target_pairs={{0,8},{8,16},{16,24},{24,32},{32,40},{40,48},{48,56},{56,64},{64,7... | collective-permute-start | bytes 393224 | tf_op jit(solution)/shard_map/ppermute | solution.py:21
  83.6 13.5 %collective-permute-start.10 = (f32[32,1024]{1,0:T(8,128)S(1)}, f32[32,1024]{1,0:T(8,128)S(1)}, u32[]{:S(2)}, u32[]{:S(2)}) collective-permute-start(f32[32,1024]{1,0:T(8,128)S(1)} %bitcast_add_fusion), channel_id=1, source_target_pairs={{0,120},{8,0},{16,8},{24,16},{32,24},{40,32},{48,40},{56,48},{64,5... | collective-permute-start | bytes 393224 | tf_op jit(solution)/shard_map/ppermute | solution.py:21

commit v3 on v2

--- a/solution.py
+++ b/solution.py
@@ -59,21 +59,28 @@
 
 
 def in_kernel(contract, place_ref, *refs):
-    *pairs, weight_ref, result_ref, high, low = refs
+    pairs, weight_ref, results, (high, low) = refs[:4], refs[4], refs[5:-2], refs[-2:]
 
     @pl.when(pl.program_id(0) == 0)
     def _():
         assemble(place_ref, pairs, high, low)
 
-    result_ref[...] = product((high[...], low[...]), halves(weight_ref[...]), contract)
-
-
-def out_kernel(pre_ref, second_ref, sum_ref):
+    result = product((high[...], low[...]), halves(weight_ref[...]), contract)
+    start = 0
+    for ref in results:
+        ref[...] = result[start : start + ref.shape[0]]
+        start += ref.shape[0]
+
+
+def out_kernel(*refs):
+    *pres, second_ref, sum_ref = refs
+
     @pl.when(pl.program_id(0) == 0)
     def _():
         sum_ref[...] = jnp.zeros_like(sum_ref)
 
-    sum_ref[...] += product(halves(gelu(pre_ref[...])), halves(second_ref[...]), PLAIN)
+    act = jnp.concatenate([gelu(ref[...]) for ref in pres])
+    sum_ref[...] += product(halves(act), halves(second_ref[...]), PLAIN)
 
 
 def back_kernel(dact_ref, old_ref, first_ref, sum_ref):
@@ -120,6 +127,33 @@
     return lax.all_to_all(value, "tensor", 0, 0, tiled=True)
 
 
+def copy_all(pairs, sems):
+    copies = [pltpu.make_async_copy(source, target, sems.at[i]) for i, (source, target) in enumerate(pairs)]
+    for copy in copies:
+        copy.start()
+    for copy in copies:
+        copy.wait()
+
+
+ANYWHERE = pl.BlockSpec(memory_space=pl.ANY)
+
+
+def placed(total, upper, *others):
+    def body(upper_ref, *refs):
+        sources, lent_ref, targets, sems = refs[: len(others)], refs[len(others)], refs[len(others) + 1 : -1], refs[-1]
+        copy_all([(upper_ref, lent_ref.at[pl.ds(0, upper.shape[0])]), *zip(sources, targets)], sems)
+
+    return pl.pallas_call(
+        body,
+        out_shape=[jax.ShapeDtypeStruct((total, upper.shape[1]), F32)]
+        + [jax.ShapeDtypeStruct(value.shape, F32) for value in others],
+        in_specs=[pl.BlockSpec(memory_space=pltpu.VMEM)] * (1 + len(others)),
+        out_specs=[ANYWHERE] * (1 + len(others)),
+        scratch_shapes=[pltpu.SemaphoreType.DMA((1 + len(others),))],
+        name="placed",
+    )(upper, *others)
+
+
 def scattered(rows, value):
     return rows + jnp.sum(exchanged(value).reshape(-1, *rows.shape), axis=0)
 
@@ -134,6 +168,7 @@
     total, depth = parts * x_rows.shape[0], x_rows.shape[1]
     wide, narrow = (total, w_first.shape[1]), (total, depth)
     scratch = [pltpu.VMEM(narrow, BF16)] * 2
+    last = total // 8
 
     def gathered(rows):
         pair = jnp.concatenate([rows, across(rows, parts // 2)])
@@ -141,22 +176,24 @@
 
     x_pairs, g_pairs = gathered(x_rows), gathered(g_rows)
     kinds = ["scalar"] + [""] * len(x_pairs)
-    (pre,) = kernel_call(
+    pres = kernel_call(
         functools.partial(in_kernel, PLAIN), "pre", 512, [place, *x_pairs, w_first], kinds + ["column"],
-        [(wide, "column")], scratch,
-    )
-    given = shifted(pre, half)
+        [((count, wide[1]), "column") for count in (total - last, last)], scratch,
+    )
+    given = [shifted(pre, half) for pre in pres]
     (d_act,) = kernel_call(
         functools.partial(in_kernel, TURNED), "dact", 512, [place, *g_pairs, w_second], kinds + ["row"],
         [(wide, "column")], scratch,
     )
-    (fwd_sum,) = kernel_call(out_kernel, "out", 512, [pre, w_second], ["column", "row"], [(narrow, "")], [])
+    (fwd_sum,) = kernel_call(out_kernel, "out", 512, [*pres, w_second], ["column"] * len(pres) + ["row"], [(narrow, "")], [])
     moved_out = shifted(scattered(x_rows, fwd_sum), 1)
     (bwd_sum,) = kernel_call(
         back_kernel, "back", 512, [d_act, old_pre, w_first], ["column", "column", "column"], [(narrow, "")], []
     )
     moved_grad = shifted(scattered(g_rows, bwd_sum), -1)
-    return (moved_out[None], moved_grad[None], given[None])
+    lent, moved_out, moved_grad = placed(total, given[0], moved_out, moved_grad)
+    lent = lax.dynamic_update_slice(lent, given[1], (total - last, 0))
+    return (moved_out[None], moved_grad[None], lent[None])
 
 
 def solution(mesh):

time: 103 us -> 98.8 us (0.959)
  waiting for transfers between devices: 21.8 us -> 15.9 us
  local copies, waits for them, and re-layouts: 4.45 us -> 1.39 us
  Pallas kernels: 30.2 us -> 33.1 us
  starting transfers between devices: 41.2 us -> 43.8 us
    unnamed x7 -> x12, local copies, waits for them, and re-layouts: 4.45 us -> 0.67 us
    all_to_all x2, waiting for transfers between devices: 6.6 us -> 3.62 us  [exchanged(): return lax.all_to_all(value, 'tensor', 0, 0, tiled=True)]
    pallas_call x0 -> x1, Pallas kernels: none -> 2.9 us  [placed(): pl.pallas_call(body, out_shape=[jax.ShapeDtypeStruct((total, upper.shape[...]
    ppermute x4 -> x5, waiting for transfers between devices: 7.11 us -> 4.27 us  [shifted(): lax.ppermute(value, 'section', [(i, (i + by) % length) for i in range(len...]
    ppermute x4 -> x5, starting transfers between devices: 14.9 us -> 17.5 us  [shifted(): lax.ppermute(value, 'section', [(i, (i + by) % length) for i in range(len...]
  transfers between devices with their start and end apart: 14 -> 15, of which waited for: 5 -> 6; matrix products, arithmetic and copies ran while one was open for 3% -> 3% of each run, Pallas kernels for 30% -> 34%
where the time goes in v3:
time: 98.8 us; the launch traced here: 98.2 us
  starting transfers between devices  43.8 us (44%)
  Pallas kernels  33.1 us (34%)
  waiting for transfers between devices  15.9 us (16%)
  other arithmetic  3.23 us (3%)
  local copies, waits for them, and re-layouts  1.39 us (1%)
    pallas_call x4, Pallas kernels, kernel_call(): pl.pallas_call(body, grid=(hidden // tile,), out_shape=[jax.ShapeDtypeStr...  30.1 us
    ppermute x5, starting transfers between devices, shifted(): lax.ppermute(value, 'section', [(i, (i + by) % length) for i in range(len...  17.5 us
    ppermute x8, starting transfers between devices, across(): return lax.ppermute(value, 'tensor', [(i, i ^ mask) for i in range(length)])  15 us
    all_to_all x2, starting transfers between devices, exchanged(): return lax.all_to_all(value, 'tensor', 0, 0, tiled=True)  11.2 us
    ppermute x8, waiting for transfers between devices, across(): return lax.ppermute(value, 'tensor', [(i, i ^ mask) for i in range(length)])  8.07 us
    ppermute x5, waiting for transfers between devices, shifted(): lax.ppermute(value, 'section', [(i, (i + by) % length) for i in range(len...  4.27 us
    all_to_all x2, waiting for transfers between devices, exchanged(): return lax.all_to_all(value, 'tensor', 0, 0, tiled=True)  3.62 us
    pallas_call x1, Pallas kernels, placed(): pl.pallas_call(body, out_shape=[jax.ShapeDtypeStruct((total, upper.shape[...  2.9 us
  transfers between devices with their start and end apart: 15, of which 6 were waited for; matrix products, arithmetic and copies ran while one was open for 3% of the time, Pallas kernels for 34%

profile of v3, /device:TPU:1, one launch (start us, length us, event | category | flops | bytes accessed | tf_op | source)
XLA Modules:
  0.0 98.2 jit_solution(13003844257474038932)
XLA Ops:
  0.6 4.5 %collective-permute-start.10 = (f32[256,2048]{1,0:T(8,128)}, f32[256,2048]{1,0:T(8,128)}, u32[]{:S(2)}, u32[]{:S(2)}) collective-permute-start(f32[256,2048]{1,0:T(8,128)} %bitcast.23), channel_id=1, source_target_pairs={{0,64},{8,72},{16,80},{24,88},{32,96},{40,104},{48,112},{56,120},{... | collective-permute-start | bytes 6291464 | tf_op jit(solution)/shard_map/ppermute | solution.py:21
  5.1 2.7 %collective-permute-start = (f32[32,1024]{1,0:T(8,128)}, f32[32,1024]{1,0:T(8,128)S(1)}, u32[]{:S(2)}, u32[]{:S(2)}) collective-permute-start(f32[32,1024]{1,0:T(8,128)} %bitcast.19), channel_id=1, source_target_pairs={{0,4},{1,5},{2,6},{3,7},{4,0},{5,1},{6,2},{7,3},{8,12},{9,13},{10,... | collective-permute-start | bytes 393224 | tf_op jit(solution)/shard_map/ppermute | solution.py:26
  7.9 3.2 %collective-permute-done = f32[32,1024]{1,0:T(8,128)S(1)} collective-permute-done((f32[32,1024]{1,0:T(8,128)}, f32[32,1024]{1,0:T(8,128)S(1)}, u32[]{:S(2)}, u32[]{:S(2)}) %collective-permute-start) | collective-permute-done | bytes 131104 | tf_op jit(solution)/shard_map/ppermute | solution.py:26
  11.1 0.9 pad_maximum_fusion.refs_0_
  12.0 2.8 %collective-permute-start.3 = (f32[64,1024]{1,0:T(8,128)S(1)}, f32[64,1024]{1,0:T(8,128)S(1)}, u32[]{:S(2)}, u32[]{:S(2)}) collective-permute-start(f32[64,1024]{1,0:T(8,128)S(1)} %pad_maximum_fusion.refs_0_), channel_id=1, source_target_pairs={{0,3},{1,2},{2,1},{3,0},{4,7},{5,6},{6,5},{7,4},{8,11},{9,10},{10,... | collective-permute-start | bytes 786440 | tf_op jit(solution)/shard_map/ppermute | solution.py:26
  14.8 0.3 collective-permute-start.2
  15.2 2.7 %collective-permute-start.6 = (f32[32,1024]{1,0:T(8,128)}, f32[32,1024]{1,0:T(8,128)S(1)}, u32[]{:S(2)}, u32[]{:S(2)}) collective-permute-start(f32[32,1024]{1,0:T(8,128)} %bitcast.21), channel_id=1, source_target_pairs={{0,4},{1,5},{2,6},{3,7},{4,0},{5,1},{6,2},{7,3},{8,12},{9,13},{10,... | collective-permute-start | bytes 393224 | tf_op jit(solution)/shard_map/ppermute | solution.py:26
  17.9 0.3 collective-permute-start.1
  18.2 2.9 %collective-permute-done.6 = f32[32,1024]{1,0:T(8,128)S(1)} collective-permute-done((f32[32,1024]{1,0:T(8,128)}, f32[32,1024]{1,0:T(8,128)S(1)}, u32[]{:S(2)}, u32[]{:S(2)}) %collective-permute-start.6) | collective-permute-done | bytes 131104 | tf_op jit(solution)/shard_map/ppermute | solution.py:26
  21.1 0.9 pad_maximum_fusion.1.refs_0_
  22.0 2.0 %collective-permute-start.9 = (f32[64,1024]{1,0:T(8,128)S(1)}, f32[64,1024]{1,0:T(8,128)S(1)}, u32[]{:S(2)}, u32[]{:S(2)}) collective-permute-start(f32[64,1024]{1,0:T(8,128)S(1)} %pad_maximum_fusion.1.refs_0_), channel_id=1, source_target_pairs={{0,3},{1,2},{2,1},{3,0},{4,7},{5,6},{6,5},{7,4},{8,11},{9,10},{10,... | collective-permute-start | bytes 786440 | tf_op jit(solution)/shard_map/ppermute | solution.py:26
  24.0 2.0 %collective-permute-done.3.refs_3_ = f32[64,1024]{1,0:T(8,128)S(1)} collective-permute-done((f32[64,1024]{1,0:T(8,128)S(1)}, f32[64,1024]{1,0:T(8,128)S(1)}, u32[]{:S(2)}, u32[]{:S(2)}) %collective-permute-start.3) | collective-permute-done | bytes 262176 | tf_op jit(solution)/shard_map/ppermute | solution.py:26
  26.0 0.8 collective-permute-start.8
  26.8 0.0 collective-permute-done.2.refs_2_
  26.8 3.3 %collective-permute-start.7 = (f32[64,1024]{1,0:T(8,128)S(1)}, f32[64,1024]{1,0:T(8,128)S(1)}, u32[]{:S(2)}, u32[]{:S(2)}) collective-permute-start(f32[64,1024]{1,0:T(8,128)S(1)} %pad_maximum_fusion.1.refs_0_), channel_id=1, source_target_pairs={{0,1},{1,0},{2,3},{3,2},{4,5},{5,4},{6,7},{7,6},{8,9},{9,8},{10,11... | collective-permute-start | bytes 786440 | tf_op jit(solution)/shard_map/ppermute | solution.py:26
  30.1 0.0 collective-permute-done.1.refs_1_
  30.1 7.4 %pre.1 = (f32[224,2048]{1,0:T(8,128)}, f32[32,2048]{1,0:T(8,128)S(1)}) custom-call(s32[1]{0:T(128)} %bitcast.place_ref, f32[64,1024]{1,0:T(8,128)S(1)} %pad_maximum_fusion.refs_0_, f32[64,1024]{1,0:T(8,128)S(1)} %collective-permute-done.1.refs_1_, f32[64,1024]{1,0:T(8,128)S(1)} %collective-permute-done.2.refs_2_, ...), custom_call_target="tpu_custom_call" | custom-call | flops 1000 | bytes 1000 | tf_op jit(solution)/shard_map/pre/pallas_call | solution.py:109
  37.5 0.0 copy-start
  37.5 0.1 collective-permute-start.4
  37.6 7.8 %out.1 = f32[256,1024]{1,0:T(8,128)} custom-call(f32[224,2048]{1,0:T(8,128)} %get-tuple-element.8.refs_0_, f32[32,2048]{1,0:T(8,128)S(1)} %get-tuple-element.9.refs_1_, f32[2048,1024]{1,0:T(8,128)} %bitcast.15), custom_call_target="tpu_custom_call" | custom-call | flops 1000 | bytes 1000 | tf_op jit(solution)/shard_map/out/pallas_call | solution.py:109
  45.4 0.0 copy-done
  45.4 4.5 %all-to-all-start = ((f32[8,32,1024]{2,1,0:T(8,128)}), f32[8,32,1024]{2,1,0:T(8,128)}, u32[]{:S(2)}, u32[]{:S(2)}) async-start(f32[8,32,1024]{2,1,0:T(8,128)} %bitcast.4), calls=%async_computation | async-start | bytes 2097152 | tf_op jit(solution)/shard_map/all_to_all | solution.py:127
  49.9 0.0 collective-permute-done.9.refs_3_
  49.9 0.0 collective-permute-done.8.refs_2_
  49.9 0.0 collective-permute-done.7.refs_1_
  49.9 6.6 %dact.1.dact_ref = f32[256,2048]{1,0:T(8,128)S(1)} custom-call(s32[1]{0:T(128)} %bitcast.place_ref, f32[64,1024]{1,0:T(8,128)S(1)} %pad_maximum_fusion.1.refs_0_, f32[64,1024]{1,0:T(8,128)S(1)} %collective-permute-done.7.refs_1_, f32[64,1024]{1,0:T(8,128)S(1)} %collective-permute-done.8.refs_2_, f32[64,1024]{1,0:T(8,128)S(1)} %collective-permute-done.9.refs_3_, ...), custom_call_target="tpu_custom_call" | custom-call | flops 1000 | bytes 1000 | tf_op jit(solution)/shard_map/dact/pallas_call | solution.py:109
  56.6 0.0 collective-permute-done.10.old_ref
  56.6 8.3 %back.1 = f32[256,1024]{1,0:T(8,128)} custom-call(f32[256,2048]{1,0:T(8,128)S(1)} %dact.1.dact_ref, f32[256,2048]{1,0:T(8,128)} %collective-permute-done.10.old_ref, f32[1024,2048]{1,0:T(8,128)} %bitcast.18), custom_call_target="tpu_custom_call" | custom-call | flops 999999995904 | bytes 1000 | tf_op jit(solution)/shard_map/back/pallas_call | solution.py:109
  64.9 0.0 copy-start.1
  64.9 0.0 copy-start.2
  64.9 0.0 all-to-all-done
  64.9 0.0 copy-start.3
  64.9 6.8 %all-to-all-start.1 = ((f32[8,32,1024]{2,1,0:T(8,128)}), f32[8,32,1024]{2,1,0:T(8,128)S(1)}, u32[]{:S(2)}, u32[]{:S(2)}) async-start(f32[8,32,1024]{2,1,0:T(8,128)} %bitcast.7), calls=%async_computation.1 | async-start | bytes 2097152 | tf_op jit(solution)/shard_map/all_to_all | solution.py:127
  71.7 0.0 copy-done.1
  71.7 2.8 %collective-permute-start.12 = (f32[32,2048]{1,0:T(8,128)S(1)}, f32[32,2048]{1,0:T(8,128)S(1)}, u32[]{:S(2)}, u32[]{:S(2)}) collective-permute-start(f32[32,2048]{1,0:T(8,128)S(1)} %copy-done.1), channel_id=1, source_target_pairs={{0,64},{8,72},{16,80},{24,88},{32,96},{40,104},{48,112},{56,120},{... | collective-permute-start | bytes 786440 | tf_op jit(solution)/shard_map/ppermute | solution.py:21
  74.5 1.3 %reduce_sum.18 = f32[32,1024]{1,0:T(8,128)S(1)} reduce(f32[8,32,1024]{2,1,0:T(8,128)} %all-to-all-done, f32[]{:T(128)} %constant.2.clone.1), dimensions={0}, to_apply=%region_0.0 | reduce | flops 229376 | bytes 1179652 | tf_op jit(solution)/shard_map/reduce_sum | solution.py:158
  75.8 0.0 copy-done.2
  75.8 4.0 %collective-permute-start.5 = (f32[32,1024]{1,0:T(8,128)S(1)}, f32[32,1024]{1,0:T(8,128)S(1)}, u32[]{:S(2)}, u32[]{:S(2)}) collective-permute-start(f32[32,1024]{1,0:T(8,128)S(1)} %bitcast_add_fusion.1), channel_id=1, source_target_pairs={{0,8},{8,16},{16,24},{24,32},{32,40},{40,48},{48,56},{56,64},{64,7... | collective-permute-start | bytes 393224 | tf_op jit(solution)/shard_map/ppermute | solution.py:21
  79.9 3.6 %all-to-all-done.1 = f32[8,32,1024]{2,1,0:T(8,128)S(1)} async-done(((f32[8,32,1024]{2,1,0:T(8,128)}), f32[8,32,1024]{2,1,0:T(8,128)S(1)}, u32[]{:S(2)}, u32[]{:S(2)}) %all-to-all-start.1) | async-done | bytes 1048608 | tf_op jit(solution)/shard_map/all_to_all | solution.py:127
  83.5 0.1 reduce_sum.19
  83.5 0.0 copy-done.3
  83.6 6.0 %collective-permute-start.11 = (f32[32,1024]{1,0:T(8,128)S(1)}, f32[32,1024]{1,0:T(8,128)S(1)}, u32[]{:S(2)}, u32[]{:S(2)}) collective-permute-start(f32[32,1024]{1,0:T(8,128)S(1)} %bitcast_add_fusion), channel_id=1, source_target_pairs={{0,120},{8,0},{16,8},{24,16},{32,24},{40,32},{48,40},{56,48},{64,5... | collective-permute-start | bytes 393224 | tf_op jit(solution)/shard_map/ppermute | solution.py:21
  89.6 0.0 collective-permute-done.5.refs_0_
  89.6 0.0 copy-start.4
  89.6 1.9 %collective-permute-done.4.upper_ref = f32[224,2048]{1,0:T(8,128)} collective-permute-done((f32[224,2048]{1,0:T(8,128)}, f32[224,2048]{1,0:T(8,128)}, u32[]{:S(2)}, u32[]{:S(2)}) %collective-permute-start.4) | collective-permute-done | bytes 1835040 | tf_op jit(solution)/shard_map/ppermute | solution.py:21
  91.5 2.3 %collective-permute-done.11.refs_1_ = f32[32,1024]{1,0:T(8,128)S(1)} collective-permute-done((f32[32,1024]{1,0:T(8,128)S(1)}, f32[32,1024]{1,0:T(8,128)S(1)}, u32[]{:S(2)}, u32[]{:S(2)}) %collective-permute-start.11) | collective-permute-done | bytes 131104 | tf_op jit(solution)/shard_map/ppermute | solution.py:21
  93.9 0.0 copy-done.4
  93.9 0.0 copy-start.5
  93.9 0.6 copy-done.5
  94.5 2.9 %placed.1 = (f32[256,2048]{1,0:T(8,128)}, f32[32,1024]{1,0:T(8,128)}, f32[32,1024]{1,0:T(8,128)}) custom-call(f32[224,2048]{1,0:T(8,128)} %collective-permute-done.4.upper_ref, f32[32,1024]{1,0:T(8,128)} %copy-done.4, f32[32,1024]{1,0:T(8,128)} %copy-done.5), custom_call_target="tpu_custom_call" | custom-call | tf_op jit(solution)/shard_map/placed/pallas_call | solution.py:146
  97.4 0.0 collective-permute-done.12
  97.4 0.7 bitcast_dynamic-update-slice_fusion
  (2 shorter events, 0.0 us)
Async XLA Ops:
  0.6 55.9 %collective-permute-start.10 = (f32[256,2048]{1,0:T(8,128)}, f32[256,2048]{1,0:T(8,128)}, u32[]{:S(2)}, u32[]{:S(2)}) collective-permute-start(f32[256,2048]{1,0:T(8,128)} %bitcast.23), channel_id=1, source_target_pairs={{0,64},{8,72},{16,80},{24,88},{32,96},{40,104},{48,112},{56,120},{... | collective-permute-start | bytes 6291464 | tf_op jit(solution)/shard_map/ppermute | solution.py:21
  5.1 5.9 %collective-permute-start = (f32[32,1024]{1,0:T(8,128)}, f32[32,1024]{1,0:T(8,128)S(1)}, u32[]{:S(2)}, u32[]{:S(2)}) collective-permute-start(f32[32,1024]{1,0:T(8,128)} %bitcast.19), channel_id=1, source_target_pairs={{0,4},{1,5},{2,6},{3,7},{4,0},{5,1},{6,2},{7,3},{8,12},{9,13},{10,... | collective-permute-start | bytes 393224 | tf_op jit(solution)/shard_map/ppermute | solution.py:26
  12.0 14.0 %collective-permute-start.3 = (f32[64,1024]{1,0:T(8,128)S(1)}, f32[64,1024]{1,0:T(8,128)S(1)}, u32[]{:S(2)}, u32[]{:S(2)}) collective-permute-start(f32[64,1024]{1,0:T(8,128)S(1)} %pad_maximum_fusion.refs_0_), channel_id=1, source_target_pairs={{0,3},{1,2},{2,1},{3,0},{4,7},{5,6},{6,5},{7,4},{8,11},{9,10},{10,... | collective-permute-start | bytes 786440 | tf_op jit(solution)/shard_map/ppermute | solution.py:26
  14.8 12.0 %collective-permute-start.2 = (f32[64,1024]{1,0:T(8,128)S(1)}, f32[64,1024]{1,0:T(8,128)S(1)}, u32[]{:S(2)}, u32[]{:S(2)}) collective-permute-start(f32[64,1024]{1,0:T(8,128)S(1)} %pad_maximum_fusion.refs_0_), channel_id=1, source_target_pairs={{0,2},{1,3},{2,0},{3,1},{4,6},{5,7},{6,4},{7,5},{8,10},{9,11},{10,... | collective-permute-start | bytes 786440 | tf_op jit(solution)/shard_map/ppermute | solution.py:26
  15.2 5.9 %collective-permute-start.6 = (f32[32,1024]{1,0:T(8,128)}, f32[32,1024]{1,0:T(8,128)S(1)}, u32[]{:S(2)}, u32[]{:S(2)}) collective-permute-start(f32[32,1024]{1,0:T(8,128)} %bitcast.21), channel_id=1, source_target_pairs={{0,4},{1,5},{2,6},{3,7},{4,0},{5,1},{6,2},{7,3},{8,12},{9,13},{10,... | collective-permute-start | bytes 393224 | tf_op jit(solution)/shard_map/ppermute | solution.py:26
  17.9 12.2 %collective-permute-start.1 = (f32[64,1024]{1,0:T(8,128)S(1)}, f32[64,1024]{1,0:T(8,128)S(1)}, u32[]{:S(2)}, u32[]{:S(2)}) collective-permute-start(f32[64,1024]{1,0:T(8,128)S(1)} %pad_maximum_fusion.refs_0_), channel_id=1, source_target_pairs={{0,1},{1,0},{2,3},{3,2},{4,5},{5,4},{6,7},{7,6},{8,9},{9,8},{10,11... | collective-permute-start | bytes 786440 | tf_op jit(solution)/shard_map/ppermute | solution.py:26
  22.0 27.9 %collective-permute-start.9 = (f32[64,1024]{1,0:T(8,128)S(1)}, f32[64,1024]{1,0:T(8,128)S(1)}, u32[]{:S(2)}, u32[]{:S(2)}) collective-permute-start(f32[64,1024]{1,0:T(8,128)S(1)} %pad_maximum_fusion.1.refs_0_), channel_id=1, source_target_pairs={{0,3},{1,2},{2,1},{3,0},{4,7},{5,6},{6,5},{7,4},{8,11},{9,10},{10,... | collective-permute-start | bytes 786440 | tf_op jit(solution)/shard_map/ppermute | solution.py:26
  26.0 23.9 %collective-permute-start.8 = (f32[64,1024]{1,0:T(8,128)S(1)}, f32[64,1024]{1,0:T(8,128)S(1)}, u32[]{:S(2)}, u32[]{:S(2)}) collective-permute-start(f32[64,1024]{1,0:T(8,128)S(1)} %pad_maximum_fusion.1.refs_0_), channel_id=1, source_target_pairs={{0,2},{1,3},{2,0},{3,1},{4,6},{5,7},{6,4},{7,5},{8,10},{9,11},{10,... | collective-permute-start | bytes 786440 | tf_op jit(solution)/shard_map/ppermute | solution.py:26
  26.8 23.1 %collective-permute-start.7 = (f32[64,1024]{1,0:T(8,128)S(1)}, f32[64,1024]{1,0:T(8,128)S(1)}, u32[]{:S(2)}, u32[]{:S(2)}) collective-permute-start(f32[64,1024]{1,0:T(8,128)S(1)} %pad_maximum_fusion.1.refs_0_), channel_id=1, source_target_pairs={{0,1},{1,0},{2,3},{3,2},{4,5},{5,4},{6,7},{7,6},{8,9},{9,8},{10,11... | collective-permute-start | bytes 786440 | tf_op jit(solution)/shard_map/ppermute | solution.py:26
  37.5 7.9 %copy-start = (f32[32,2048]{1,0:T(8,128)}, f32[32,2048]{1,0:T(8,128)S(1)}, u32[]{:S(2)}) copy-start(f32[32,2048]{1,0:T(8,128)S(1)} %get-tuple-element.9.refs_1_) | copy-start | bytes 786436
  37.5 54.0 %collective-permute-start.4 = (f32[224,2048]{1,0:T(8,128)}, f32[224,2048]{1,0:T(8,128)}, u32[]{:S(2)}, u32[]{:S(2)}) collective-permute-start(f32[224,2048]{1,0:T(8,128)} %get-tuple-element.8.refs_0_), channel_id=1, source_target_pairs={{0,64},{8,72},{16,80},{24,88},{32,96},{40,104},{48,112},{56,120},{... | collective-permute-start | bytes 5505032 | tf_op jit(solution)/shard_map/ppermute | solution.py:21
  45.4 19.5 %all-to-all-start = ((f32[8,32,1024]{2,1,0:T(8,128)}), f32[8,32,1024]{2,1,0:T(8,128)}, u32[]{:S(2)}, u32[]{:S(2)}) async-start(f32[8,32,1024]{2,1,0:T(8,128)} %bitcast.4), calls=%async_computation | async-start | bytes 2097152 | tf_op jit(solution)/shard_map/all_to_all | solution.py:127
  64.9 6.8 %copy-start.1 = (f32[32,2048]{1,0:T(8,128)S(1)}, f32[32,2048]{1,0:T(8,128)}, u32[]{:S(2)}) copy-start(f32[32,2048]{1,0:T(8,128)} %copy-done) | copy-start | bytes 786436
  64.9 10.9 %copy-start.2 = (f32[1,32,1024]{2,1,0:T(8,128)S(1)}, f32[1,32,1024]{2,1,0:T(8,128)}, u32[]{:S(2)}) copy-start(f32[1,32,1024]{2,1,0:T(8,128)} %param.5) | copy-start | bytes 393220
  64.9 18.7 %copy-start.3 = (f32[1,32,1024]{2,1,0:T(8,128)S(1)}, f32[1,32,1024]{2,1,0:T(8,128)}, u32[]{:S(2)}) copy-start(f32[1,32,1024]{2,1,0:T(8,128)} %param.6) | copy-start | bytes 393220
  64.9 18.6 %all-to-all-start.1 = ((f32[8,32,1024]{2,1,0:T(8,128)}), f32[8,32,1024]{2,1,0:T(8,128)S(1)}, u32[]{:S(2)}, u32[]{:S(2)}) async-start(f32[8,32,1024]{2,1,0:T(8,128)} %bitcast.7), calls=%async_computation.1 | async-start | bytes 2097152 | tf_op jit(solution)/shard_map/all_to_all | solution.py:127
  71.7 25.7 %collective-permute-start.12 = (f32[32,2048]{1,0:T(8,128)S(1)}, f32[32,2048]{1,0:T(8,128)S(1)}, u32[]{:S(2)}, u32[]{:S(2)}) collective-permute-start(f32[32,2048]{1,0:T(8,128)S(1)} %copy-done.1), channel_id=1, source_target_pairs={{0,64},{8,72},{16,80},{24,88},{32,96},{40,104},{48,112},{56,120},{... | collective-permute-start | bytes 786440 | tf_op jit(solution)/shard_map/ppermute | solution.py:21
  75.8 13.8 %collective-permute-start.5 = (f32[32,1024]{1,0:T(8,128)S(1)}, f32[32,1024]{1,0:T(8,128)S(1)}, u32[]{:S(2)}, u32[]{:S(2)}) collective-permute-start(f32[32,1024]{1,0:T(8,128)S(1)} %bitcast_add_fusion.1), channel_id=1, source_target_pairs={{0,8},{8,16},{16,24},{24,32},{32,40},{40,48},{48,56},{56,64},{64,7... | collective-permute-start | bytes 393224 | tf_op jit(solution)/shard_map/ppermute | solution.py:21
  83.6 10.3 %collective-permute-start.11 = (f32[32,1024]{1,0:T(8,128)S(1)}, f32[32,1024]{1,0:T(8,128)S(1)}, u32[]{:S(2)}, u32[]{:S(2)}) collective-permute-start(f32[32,1024]{1,0:T(8,128)S(1)} %bitcast_add_fusion), channel_id=1, source_target_pairs={{0,120},{8,0},{16,8},{24,16},{32,24},{40,32},{48,40},{56,48},{64,5... | collective-permute-start | bytes 393224 | tf_op jit(solution)/shard_map/ppermute | solution.py:21
  89.6 4.3 %copy-start.4 = (f32[32,1024]{1,0:T(8,128)}, f32[32,1024]{1,0:T(8,128)S(1)}, u32[]{:S(2)}) copy-start(f32[32,1024]{1,0:T(8,128)S(1)} %collective-permute-done.5.refs_0_) | copy-start | bytes 393220
  93.9 0.6 copy-start.5

commit v4 on v3

--- a/solution.py
+++ b/solution.py
@@ -150,6 +150,7 @@
         in_specs=[pl.BlockSpec(memory_space=pltpu.VMEM)] * (1 + len(others)),
         out_specs=[ANYWHERE] * (1 + len(others)),
         scratch_shapes=[pltpu.SemaphoreType.DMA((1 + len(others),))],
+        compiler_params=pltpu.CompilerParams(vmem_limit_bytes=8 * 1024 * 1024),
         name="placed",
     )(upper, *others)
 

time: 98.8 us -> 98.8 us (level)
  transfers between devices with their start and end apart: 15 -> 15, of which waited for: 6 -> 7; matrix products, arithmetic and copies ran while one was open for 3% -> 3% of each run, Pallas kernels for 34% -> 34%
where the time goes in v4:
time: 98.8 us; the launch traced here: 97.8 us
  starting transfers between devices  43.8 us (44%)
  Pallas kernels  33 us (33%)
  waiting for transfers between devices  16.3 us (16%)
  other arithmetic  3.23 us (3%)
    pallas_call x4, Pallas kernels, kernel_call(): pl.pallas_call(body, grid=(hidden // tile,), out_shape=[jax.ShapeDtypeStr...  30.1 us
    ppermute x5, starting transfers between devices, shifted(): lax.ppermute(value, 'section', [(i, (i + by) % length) for i in range(len...  17.5 us
    ppermute x8, starting transfers between devices, across(): return lax.ppermute(value, 'tensor', [(i, i ^ mask) for i in range(length)])  15 us
    all_to_all x2, starting transfers between devices, exchanged(): return lax.all_to_all(value, 'tensor', 0, 0, tiled=True)  11.2 us
    ppermute x8, waiting for transfers between devices, across(): return lax.ppermute(value, 'tensor', [(i, i ^ mask) for i in range(length)])  8.07 us
    ppermute x5, waiting for transfers between devices, shifted(): lax.ppermute(value, 'section', [(i, (i + by) % length) for i in range(len...  4.63 us
    all_to_all x2, waiting for transfers between devices, exchanged(): return lax.all_to_all(value, 'tensor', 0, 0, tiled=True)  3.6 us
    pallas_call x1, Pallas kernels, placed(): pl.pallas_call(body, out_shape=[jax.ShapeDtypeStruct((total, upper.shape[...  2.83 us
  transfers between devices with their start and end apart: 15, of which 7 were waited for; matrix products, arithmetic and copies ran while one was open for 3% of the time, Pallas kernels for 34%

profile of v4, /device:TPU:1, one launch (start us, length us, event | category | flops | bytes accessed | tf_op | source)
XLA Modules:
  0.0 97.8 jit_solution(1572951266798312700)
XLA Ops:
  0.6 4.5 %collective-permute-start.10 = (f32[256,2048]{1,0:T(8,128)}, f32[256,2048]{1,0:T(8,128)}, u32[]{:S(2)}, u32[]{:S(2)}) collective-permute-start(f32[256,2048]{1,0:T(8,128)} %bitcast.23), channel_id=1, source_target_pairs={{0,64},{8,72},{16,80},{24,88},{32,96},{40,104},{48,112},{56,120},{... | collective-permute-start | bytes 6291464 | tf_op jit(solution)/shard_map/ppermute | solution.py:21
  5.1 2.7 %collective-permute-start = (f32[32,1024]{1,0:T(8,128)}, f32[32,1024]{1,0:T(8,128)S(1)}, u32[]{:S(2)}, u32[]{:S(2)}) collective-permute-start(f32[32,1024]{1,0:T(8,128)} %bitcast.19), channel_id=1, source_target_pairs={{0,4},{1,5},{2,6},{3,7},{4,0},{5,1},{6,2},{7,3},{8,12},{9,13},{10,... | collective-permute-start | bytes 393224 | tf_op jit(solution)/shard_map/ppermute | solution.py:26
  7.9 3.2 %collective-permute-done = f32[32,1024]{1,0:T(8,128)S(1)} collective-permute-done((f32[32,1024]{1,0:T(8,128)}, f32[32,1024]{1,0:T(8,128)S(1)}, u32[]{:S(2)}, u32[]{:S(2)}) %collective-permute-start) | collective-permute-done | bytes 131104 | tf_op jit(solution)/shard_map/ppermute | solution.py:26
  11.1 0.9 pad_maximum_fusion.refs_0_
  12.0 2.8 %collective-permute-start.3 = (f32[64,1024]{1,0:T(8,128)S(1)}, f32[64,1024]{1,0:T(8,128)S(1)}, u32[]{:S(2)}, u32[]{:S(2)}) collective-permute-start(f32[64,1024]{1,0:T(8,128)S(1)} %pad_maximum_fusion.refs_0_), channel_id=1, source_target_pairs={{0,3},{1,2},{2,1},{3,0},{4,7},{5,6},{6,5},{7,4},{8,11},{9,10},{10,... | collective-permute-start | bytes 786440 | tf_op jit(solution)/shard_map/ppermute | solution.py:26
  14.8 0.3 collective-permute-start.2
  15.2 2.7 %collective-permute-start.6 = (f32[32,1024]{1,0:T(8,128)}, f32[32,1024]{1,0:T(8,128)S(1)}, u32[]{:S(2)}, u32[]{:S(2)}) collective-permute-start(f32[32,1024]{1,0:T(8,128)} %bitcast.21), channel_id=1, source_target_pairs={{0,4},{1,5},{2,6},{3,7},{4,0},{5,1},{6,2},{7,3},{8,12},{9,13},{10,... | collective-permute-start | bytes 393224 | tf_op jit(solution)/shard_map/ppermute | solution.py:26
  17.9 0.3 collective-permute-start.1
  18.2 2.9 %collective-permute-done.6 = f32[32,1024]{1,0:T(8,128)S(1)} collective-permute-done((f32[32,1024]{1,0:T(8,128)}, f32[32,1024]{1,0:T(8,128)S(1)}, u32[]{:S(2)}, u32[]{:S(2)}) %collective-permute-start.6) | collective-permute-done | bytes 131104 | tf_op jit(solution)/shard_map/ppermute | solution.py:26
  21.1 0.9 pad_maximum_fusion.1.refs_0_
  22.0 2.0 %collective-permute-start.9 = (f32[64,1024]{1,0:T(8,128)S(1)}, f32[64,1024]{1,0:T(8,128)S(1)}, u32[]{:S(2)}, u32[]{:S(2)}) collective-permute-start(f32[64,1024]{1,0:T(8,128)S(1)} %pad_maximum_fusion.1.refs_0_), channel_id=1, source_target_pairs={{0,3},{1,2},{2,1},{3,0},{4,7},{5,6},{6,5},{7,4},{8,11},{9,10},{10,... | collective-permute-start | bytes 786440 | tf_op jit(solution)/shard_map/ppermute | solution.py:26
  24.0 2.0 %collective-permute-done.3.refs_3_ = f32[64,1024]{1,0:T(8,128)S(1)} collective-permute-done((f32[64,1024]{1,0:T(8,128)S(1)}, f32[64,1024]{1,0:T(8,128)S(1)}, u32[]{:S(2)}, u32[]{:S(2)}) %collective-permute-start.3) | collective-permute-done | bytes 262176 | tf_op jit(solution)/shard_map/ppermute | solution.py:26
  26.0 0.8 collective-permute-start.8
  26.8 0.0 collective-permute-done.2.refs_2_
  26.8 3.3 %collective-permute-start.7 = (f32[64,1024]{1,0:T(8,128)S(1)}, f32[64,1024]{1,0:T(8,128)S(1)}, u32[]{:S(2)}, u32[]{:S(2)}) collective-permute-start(f32[64,1024]{1,0:T(8,128)S(1)} %pad_maximum_fusion.1.refs_0_), channel_id=1, source_target_pairs={{0,1},{1,0},{2,3},{3,2},{4,5},{5,4},{6,7},{7,6},{8,9},{9,8},{10,11... | collective-permute-start | bytes 786440 | tf_op jit(solution)/shard_map/ppermute | solution.py:26
  30.1 0.0 collective-permute-done.1.refs_1_
  30.1 7.4 %pre.1 = (f32[224,2048]{1,0:T(8,128)}, f32[32,2048]{1,0:T(8,128)S(1)}) custom-call(s32[1]{0:T(128)} %bitcast.place_ref, f32[64,1024]{1,0:T(8,128)S(1)} %pad_maximum_fusion.refs_0_, f32[64,1024]{1,0:T(8,128)S(1)} %collective-permute-done.1.refs_1_, f32[64,1024]{1,0:T(8,128)S(1)} %collective-permute-done.2.refs_2_, ...), custom_call_target="tpu_custom_call" | custom-call | flops 1000 | bytes 1000 | tf_op jit(solution)/shard_map/pre/pallas_call | solution.py:109
  37.5 0.0 copy-start
  37.5 0.1 collective-permute-start.4
  37.6 7.8 %out.1 = f32[256,1024]{1,0:T(8,128)} custom-call(f32[224,2048]{1,0:T(8,128)} %get-tuple-element.8.refs_0_, f32[32,2048]{1,0:T(8,128)S(1)} %get-tuple-element.9.refs_1_, f32[2048,1024]{1,0:T(8,128)} %bitcast.15), custom_call_target="tpu_custom_call" | custom-call | flops 1000 | bytes 1000 | tf_op jit(solution)/shard_map/out/pallas_call | solution.py:109
  45.4 0.0 copy-done
  45.4 4.5 %all-to-all-start = ((f32[8,32,1024]{2,1,0:T(8,128)}), f32[8,32,1024]{2,1,0:T(8,128)}, u32[]{:S(2)}, u32[]{:S(2)}) async-start(f32[8,32,1024]{2,1,0:T(8,128)} %bitcast.4), calls=%async_computation | async-start | bytes 2097152 | tf_op jit(solution)/shard_map/all_to_all | solution.py:127
  49.9 0.0 collective-permute-done.9.refs_3_
  49.9 0.0 collective-permute-done.8.refs_2_
  49.9 0.0 collective-permute-done.7.refs_1_
  49.9 6.6 %dact.1.dact_ref = f32[256,2048]{1,0:T(8,128)S(1)} custom-call(s32[1]{0:T(128)} %bitcast.place_ref, f32[64,1024]{1,0:T(8,128)S(1)} %pad_maximum_fusion.1.refs_0_, f32[64,1024]{1,0:T(8,128)S(1)} %collective-permute-done.7.refs_1_, f32[64,1024]{1,0:T(8,128)S(1)} %collective-permute-done.8.refs_2_, f32[64,1024]{1,0:T(8,128)S(1)} %collective-permute-done.9.refs_3_, ...), custom_call_target="tpu_custom_call" | custom-call | flops 1000 | bytes 1000 | tf_op jit(solution)/shard_map/dact/pallas_call | solution.py:109
  56.5 0.0 collective-permute-done.10.old_ref
  56.6 8.3 %back.1 = f32[256,1024]{1,0:T(8,128)} custom-call(f32[256,2048]{1,0:T(8,128)S(1)} %dact.1.dact_ref, f32[256,2048]{1,0:T(8,128)} %collective-permute-done.10.old_ref, f32[1024,2048]{1,0:T(8,128)} %bitcast.18), custom_call_target="tpu_custom_call" | custom-call | flops 999999995904 | bytes 1000 | tf_op jit(solution)/shard_map/back/pallas_call | solution.py:109
  64.9 0.0 copy-start.1
  64.9 0.0 copy-start.2
  64.9 0.0 all-to-all-done
  64.9 0.0 copy-start.3
  64.9 6.8 %all-to-all-start.1 = ((f32[8,32,1024]{2,1,0:T(8,128)}), f32[8,32,1024]{2,1,0:T(8,128)S(1)}, u32[]{:S(2)}, u32[]{:S(2)}) async-start(f32[8,32,1024]{2,1,0:T(8,128)} %bitcast.7), calls=%async_computation.1 | async-start | bytes 2097152 | tf_op jit(solution)/shard_map/all_to_all | solution.py:127
  71.7 0.0 copy-done.1
  71.7 2.8 %collective-permute-start.12 = (f32[32,2048]{1,0:T(8,128)S(1)}, f32[32,2048]{1,0:T(8,128)S(1)}, u32[]{:S(2)}, u32[]{:S(2)}) collective-permute-start(f32[32,2048]{1,0:T(8,128)S(1)} %copy-done.1), channel_id=1, source_target_pairs={{0,64},{8,72},{16,80},{24,88},{32,96},{40,104},{48,112},{56,120},{... | collective-permute-start | bytes 786440 | tf_op jit(solution)/shard_map/ppermute | solution.py:21
  74.5 1.3 %reduce_sum.18 = f32[32,1024]{1,0:T(8,128)S(1)} reduce(f32[8,32,1024]{2,1,0:T(8,128)} %all-to-all-done, f32[]{:T(128)} %constant.2.clone.1), dimensions={0}, to_apply=%region_0.0 | reduce | flops 229376 | bytes 1179652 | tf_op jit(solution)/shard_map/reduce_sum | solution.py:159
  75.8 0.0 copy-done.2
  75.8 4.1 %collective-permute-start.5 = (f32[32,1024]{1,0:T(8,128)S(1)}, f32[32,1024]{1,0:T(8,128)S(1)}, u32[]{:S(2)}, u32[]{:S(2)}) collective-permute-start(f32[32,1024]{1,0:T(8,128)S(1)} %bitcast_add_fusion.1), channel_id=1, source_target_pairs={{0,8},{8,16},{16,24},{24,32},{32,40},{40,48},{48,56},{56,64},{64,7... | collective-permute-start | bytes 393224 | tf_op jit(solution)/shard_map/ppermute | solution.py:21
  79.9 3.6 %all-to-all-done.1 = f32[8,32,1024]{2,1,0:T(8,128)S(1)} async-done(((f32[8,32,1024]{2,1,0:T(8,128)}), f32[8,32,1024]{2,1,0:T(8,128)S(1)}, u32[]{:S(2)}, u32[]{:S(2)}) %all-to-all-start.1) | async-done | bytes 1048608 | tf_op jit(solution)/shard_map/all_to_all | solution.py:127
  83.5 0.1 reduce_sum.19
  83.6 0.0 copy-done.3
  83.6 6.0 %collective-permute-start.11 = (f32[32,1024]{1,0:T(8,128)S(1)}, f32[32,1024]{1,0:T(8,128)S(1)}, u32[]{:S(2)}, u32[]{:S(2)}) collective-permute-start(f32[32,1024]{1,0:T(8,128)S(1)} %bitcast_add_fusion), channel_id=1, source_target_pairs={{0,120},{8,0},{16,8},{24,16},{32,24},{40,32},{48,40},{56,48},{64,5... | collective-permute-start | bytes 393224 | tf_op jit(solution)/shard_map/ppermute | solution.py:21
  89.6 0.0 collective-permute-done.5.refs_0_
  89.6 1.9 %collective-permute-done.4.upper_ref = f32[224,2048]{1,0:T(8,128)} collective-permute-done((f32[224,2048]{1,0:T(8,128)}, f32[224,2048]{1,0:T(8,128)}, u32[]{:S(2)}, u32[]{:S(2)}) %collective-permute-start.4) | collective-permute-done | bytes 1835040 | tf_op jit(solution)/shard_map/ppermute | solution.py:21
  91.5 2.3 %collective-permute-done.11.refs_1_ = f32[32,1024]{1,0:T(8,128)S(1)} collective-permute-done((f32[32,1024]{1,0:T(8,128)S(1)}, f32[32,1024]{1,0:T(8,128)S(1)}, u32[]{:S(2)}, u32[]{:S(2)}) %collective-permute-start.11) | collective-permute-done | bytes 131104 | tf_op jit(solution)/shard_map/ppermute | solution.py:21
  93.9 2.8 %placed.1 = (f32[256,2048]{1,0:T(8,128)}, f32[32,1024]{1,0:T(8,128)}, f32[32,1024]{1,0:T(8,128)}) custom-call(f32[224,2048]{1,0:T(8,128)} %collective-permute-done.4.upper_ref, f32[32,1024]{1,0:T(8,128)S(1)} %collective-permute-done.5.refs_0_, f32[32,1024]{1,0:T(8,128)S(1)} %collective-permute-done.11.refs_1_), custom_call_target="tpu_custom_call" | custom-call | tf_op jit(solution)/shard_map/placed/pallas_call | solution.py:146
  96.7 0.3 collective-permute-done.12
  97.0 0.7 bitcast_dynamic-update-slice_fusion
  (2 shorter events, 0.0 us)
Async XLA Ops:
  0.6 55.9 %collective-permute-start.10 = (f32[256,2048]{1,0:T(8,128)}, f32[256,2048]{1,0:T(8,128)}, u32[]{:S(2)}, u32[]{:S(2)}) collective-permute-start(f32[256,2048]{1,0:T(8,128)} %bitcast.23), channel_id=1, source_target_pairs={{0,64},{8,72},{16,80},{24,88},{32,96},{40,104},{48,112},{56,120},{... | collective-permute-start | bytes 6291464 | tf_op jit(solution)/shard_map/ppermute | solution.py:21
  5.1 5.9 %collective-permute-start = (f32[32,1024]{1,0:T(8,128)}, f32[32,1024]{1,0:T(8,128)S(1)}, u32[]{:S(2)}, u32[]{:S(2)}) collective-permute-start(f32[32,1024]{1,0:T(8,128)} %bitcast.19), channel_id=1, source_target_pairs={{0,4},{1,5},{2,6},{3,7},{4,0},{5,1},{6,2},{7,3},{8,12},{9,13},{10,... | collective-permute-start | bytes 393224 | tf_op jit(solution)/shard_map/ppermute | solution.py:26
  12.0 14.0 %collective-permute-start.3 = (f32[64,1024]{1,0:T(8,128)S(1)}, f32[64,1024]{1,0:T(8,128)S(1)}, u32[]{:S(2)}, u32[]{:S(2)}) collective-permute-start(f32[64,1024]{1,0:T(8,128)S(1)} %pad_maximum_fusion.refs_0_), channel_id=1, source_target_pairs={{0,3},{1,2},{2,1},{3,0},{4,7},{5,6},{6,5},{7,4},{8,11},{9,10},{10,... | collective-permute-start | bytes 786440 | tf_op jit(solution)/shard_map/ppermute | solution.py:26
  14.8 12.0 %collective-permute-start.2 = (f32[64,1024]{1,0:T(8,128)S(1)}, f32[64,1024]{1,0:T(8,128)S(1)}, u32[]{:S(2)}, u32[]{:S(2)}) collective-permute-start(f32[64,1024]{1,0:T(8,128)S(1)} %pad_maximum_fusion.refs_0_), channel_id=1, source_target_pairs={{0,2},{1,3},{2,0},{3,1},{4,6},{5,7},{6,4},{7,5},{8,10},{9,11},{10,... | collective-permute-start | bytes 786440 | tf_op jit(solution)/shard_map/ppermute | solution.py:26
  15.2 5.9 %collective-permute-start.6 = (f32[32,1024]{1,0:T(8,128)}, f32[32,1024]{1,0:T(8,128)S(1)}, u32[]{:S(2)}, u32[]{:S(2)}) collective-permute-start(f32[32,1024]{1,0:T(8,128)} %bitcast.21), channel_id=1, source_target_pairs={{0,4},{1,5},{2,6},{3,7},{4,0},{5,1},{6,2},{7,3},{8,12},{9,13},{10,... | collective-permute-start | bytes 393224 | tf_op jit(solution)/shard_map/ppermute | solution.py:26
  17.9 12.2 %collective-permute-start.1 = (f32[64,1024]{1,0:T(8,128)S(1)}, f32[64,1024]{1,0:T(8,128)S(1)}, u32[]{:S(2)}, u32[]{:S(2)}) collective-permute-start(f32[64,1024]{1,0:T(8,128)S(1)} %pad_maximum_fusion.refs_0_), channel_id=1, source_target_pairs={{0,1},{1,0},{2,3},{3,2},{4,5},{5,4},{6,7},{7,6},{8,9},{9,8},{10,11... | collective-permute-start | bytes 786440 | tf_op jit(solution)/shard_map/ppermute | solution.py:26
  22.0 27.9 %collective-permute-start.9 = (f32[64,1024]{1,0:T(8,128)S(1)}, f32[64,1024]{1,0:T(8,128)S(1)}, u32[]{:S(2)}, u32[]{:S(2)}) collective-permute-start(f32[64,1024]{1,0:T(8,128)S(1)} %pad_maximum_fusion.1.refs_0_), channel_id=1, source_target_pairs={{0,3},{1,2},{2,1},{3,0},{4,7},{5,6},{6,5},{7,4},{8,11},{9,10},{10,... | collective-permute-start | bytes 786440 | tf_op jit(solution)/shard_map/ppermute | solution.py:26
  26.0 23.9 %collective-permute-start.8 = (f32[64,1024]{1,0:T(8,128)S(1)}, f32[64,1024]{1,0:T(8,128)S(1)}, u32[]{:S(2)}, u32[]{:S(2)}) collective-permute-start(f32[64,1024]{1,0:T(8,128)S(1)} %pad_maximum_fusion.1.refs_0_), channel_id=1, source_target_pairs={{0,2},{1,3},{2,0},{3,1},{4,6},{5,7},{6,4},{7,5},{8,10},{9,11},{10,... | collective-permute-start | bytes 786440 | tf_op jit(solution)/shard_map/ppermute | solution.py:26
  26.8 23.1 %collective-permute-start.7 = (f32[64,1024]{1,0:T(8,128)S(1)}, f32[64,1024]{1,0:T(8,128)S(1)}, u32[]{:S(2)}, u32[]{:S(2)}) collective-permute-start(f32[64,1024]{1,0:T(8,128)S(1)} %pad_maximum_fusion.1.refs_0_), channel_id=1, source_target_pairs={{0,1},{1,0},{2,3},{3,2},{4,5},{5,4},{6,7},{7,6},{8,9},{9,8},{10,11... | collective-permute-start | bytes 786440 | tf_op jit(solution)/shard_map/ppermute | solution.py:26
  37.5 7.9 %copy-start = (f32[32,2048]{1,0:T(8,128)}, f32[32,2048]{1,0:T(8,128)S(1)}, u32[]{:S(2)}) copy-start(f32[32,2048]{1,0:T(8,128)S(1)} %get-tuple-element.9.refs_1_) | copy-start | bytes 786436
  37.5 54.0 %collective-permute-start.4 = (f32[224,2048]{1,0:T(8,128)}, f32[224,2048]{1,0:T(8,128)}, u32[]{:S(2)}, u32[]{:S(2)}) collective-permute-start(f32[224,2048]{1,0:T(8,128)} %get-tuple-element.8.refs_0_), channel_id=1, source_target_pairs={{0,64},{8,72},{16,80},{24,88},{32,96},{40,104},{48,112},{56,120},{... | collective-permute-start | bytes 5505032 | tf_op jit(solution)/shard_map/ppermute | solution.py:21
  45.4 19.5 %all-to-all-start = ((f32[8,32,1024]{2,1,0:T(8,128)}), f32[8,32,1024]{2,1,0:T(8,128)}, u32[]{:S(2)}, u32[]{:S(2)}) async-start(f32[8,32,1024]{2,1,0:T(8,128)} %bitcast.4), calls=%async_computation | async-start | bytes 2097152 | tf_op jit(solution)/shard_map/all_to_all | solution.py:127
  64.9 6.8 %copy-start.1 = (f32[32,2048]{1,0:T(8,128)S(1)}, f32[32,2048]{1,0:T(8,128)}, u32[]{:S(2)}) copy-start(f32[32,2048]{1,0:T(8,128)} %copy-done) | copy-start | bytes 786436
  64.9 10.9 %copy-start.2 = (f32[1,32,1024]{2,1,0:T(8,128)S(1)}, f32[1,32,1024]{2,1,0:T(8,128)}, u32[]{:S(2)}) copy-start(f32[1,32,1024]{2,1,0:T(8,128)} %param.5) | copy-start | bytes 393220
  64.9 18.7 %copy-start.3 = (f32[1,32,1024]{2,1,0:T(8,128)S(1)}, f32[1,32,1024]{2,1,0:T(8,128)}, u32[]{:S(2)}) copy-start(f32[1,32,1024]{2,1,0:T(8,128)} %param.6) | copy-start | bytes 393220
  64.9 18.6 %all-to-all-start.1 = ((f32[8,32,1024]{2,1,0:T(8,128)}), f32[8,32,1024]{2,1,0:T(8,128)S(1)}, u32[]{:S(2)}, u32[]{:S(2)}) async-start(f32[8,32,1024]{2,1,0:T(8,128)} %bitcast.7), calls=%async_computation.1 | async-start | bytes 2097152 | tf_op jit(solution)/shard_map/all_to_all | solution.py:127
  71.7 25.4 %collective-permute-start.12 = (f32[32,2048]{1,0:T(8,128)S(1)}, f32[32,2048]{1,0:T(8,128)S(1)}, u32[]{:S(2)}, u32[]{:S(2)}) collective-permute-start(f32[32,2048]{1,0:T(8,128)S(1)} %copy-done.1), channel_id=1, source_target_pairs={{0,64},{8,72},{16,80},{24,88},{32,96},{40,104},{48,112},{56,120},{... | collective-permute-start | bytes 786440 | tf_op jit(solution)/shard_map/ppermute | solution.py:21
  75.8 13.8 %collective-permute-start.5 = (f32[32,1024]{1,0:T(8,128)S(1)}, f32[32,1024]{1,0:T(8,128)S(1)}, u32[]{:S(2)}, u32[]{:S(2)}) collective-permute-start(f32[32,1024]{1,0:T(8,128)S(1)} %bitcast_add_fusion.1), channel_id=1, source_target_pairs={{0,8},{8,16},{16,24},{24,32},{32,40},{40,48},{48,56},{56,64},{64,7... | collective-permute-start | bytes 393224 | tf_op jit(solution)/shard_map/ppermute | solution.py:21
  83.6 10.3 %collective-permute-start.11 = (f32[32,1024]{1,0:T(8,128)S(1)}, f32[32,1024]{1,0:T(8,128)S(1)}, u32[]{:S(2)}, u32[]{:S(2)}) collective-permute-start(f32[32,1024]{1,0:T(8,128)S(1)} %bitcast_add_fusion), channel_id=1, source_target_pairs={{0,120},{8,0},{16,8},{24,16},{32,24},{40,32},{48,40},{56,48},{64,5... | collective-permute-start | bytes 393224 | tf_op jit(solution)/shard_map/ppermute | solution.py:21
